TPU v7x, 32 devices: a whole 2x2x4 slice. The times are simulated.
32 devices in a mesh: head: 4 (over z), tok: 8 (over y, x, core).
Axes of the slice: x: 2, y: 2, z: 4, core: 2. Of those that a mesh axis runs over, the one named last changes fastest.
Arguments:
- teacher_q: bfloat16 [1024, 1024], P('tok', 'head'), may hold values from -48 to 48
- student_q: bfloat16 [1024, 1024], P('tok', 'head'), may hold values from -48 to 48
- owner_table: int32 [8, 8], replicated, may hold values from -1 to 7, as said below
Outputs:
- student_grad: bfloat16 [1024, 1024], P('tok', 'head')
- divergence: float32 [16], P('head')
Inputs may be any that keep to these rules, and one draw needn't show every extreme that they name: `owner_table`: Symmetric; every diagonal entry is an owner; an owner is a tok index; each tok index owns at most 2 pairs i <= j, and some tok index owns exactly 2 in every draw.
All inputs are finite; a program needn't handle non-finite values.
Results may differ from a plain program's by a relative error of at most 0.0049.
Values may be sent and summed in bfloat16 or wider, within the bound.
A program may use at most 64 MiB of HBM per device.

v0:
```python
import functools
import math

import jax
import jax.numpy as jnp
from jax import lax
from jax.experimental import pallas as pl
from jax.experimental.pallas import tpu as pltpu
from jax.sharding import PartitionSpec as P

HEAD_DIM = 64
LANES = 128
floor_value = -1e30
distill_weight = 32.0
score_factor = HEAD_DIM ** (-0.5) * math.log2(math.e)
MESH = pl.DeviceIdType.MESH


def repeat(count, body, init=None):
    if count <= 8:
        for step in range(count):
            init = body(step, init)
        return init
    return lax.fori_loop(0, count, body, init)


def kernel(
    n, teacher_hbm, student_hbm, table, in_grad, in_div,
    teacher, student, outbox, inbox, own, scores, top, logs, row_part, stats,
    out_grad, out_div, local_sem, send_sem, recv_sem, stat_send, stat_recv, back_send, back_recv,
):
    rows, width = teacher_hbm.shape
    pairs = width // LANES
    heads = width // HEAD_DIM
    group = LANES // HEAD_DIM
    parts = n // heads
    chips = n // 2
    side = math.isqrt(chips)
    side = side if side * side == chips else 1
    span = chips // side
    half = rows // 2
    own_rows = heads * rows
    me = lax.axis_index("tok")
    head_at = lax.axis_index("head")
    chip, core = me // 2, me % 2
    head, part = me // parts, me % parts

    def spot(tok):
        return (head_at, tok)

    def shifted(k, sign):
        high = (chip // span + sign * (k // span) + side) % side
        low = (chip % span + sign * (k % span) + span) % span
        return high * span + low

    def remote(src, dst, send, recv, target):
        return pltpu.make_async_remote_copy(
            src_ref=src, dst_ref=dst, send_sem=send, recv_sem=recv,
            device_id=spot(target), device_id_type=MESH,
        )

    barrier = pltpu.get_barrier_semaphore()
    loads = [
        pltpu.make_async_copy(teacher_hbm, teacher, local_sem.at[0]),
        pltpu.make_async_copy(student_hbm, student, local_sem.at[1]),
    ]
    for load in loads:
        load.start()

    def greet(d, carry):
        pl.semaphore_signal(barrier, inc=1, device_id=spot((me + d + 1) % n), device_id_type=MESH)
        return carry

    repeat(n - 1, greet)
    for load in loads:
        load.wait()
    lane = lax.broadcasted_iota(jnp.int32, (rows, LANES), 1)
    lower = lane < HEAD_DIM
    for pair in range(pairs):
        columns = pl.ds(pair * LANES, LANES)
        t_pair = teacher[:, columns].astype(jnp.float32)
        s_pair = student[:, columns].astype(jnp.float32)
        outbox[pair * group] = jnp.where(lower, t_pair, pltpu.roll(s_pair, HEAD_DIM, 1)).astype(
            jnp.bfloat16
        )
        outbox[pair * group + 1] = jnp.where(
            lower, pltpu.roll(t_pair, HEAD_DIM, 1), s_pair
        ).astype(jnp.bfloat16)
    inbox[pl.ds(me * rows, rows), :] = outbox[head]
    pl.semaphore_wait(barrier, n - 1)

    def query_copy(k, other, target):
        return remote(
            outbox.at[target // parts],
            inbox.at[pl.ds(me * rows, rows), :],
            send_sem.at[k, other],
            recv_sem.at[k, other],
            target,
        )

    def away(k, other, sign):
        return shifted(k, sign) * 2 + (1 - core if other else core)

    def send_queries(step, carry):
        k = chips - 1 - step
        for other in range(2):
            query_copy(k, other, away(k, other, 1)).start()
        return carry

    repeat(chips - 1, send_queries)
    query_copy(0, 1, away(0, 1, 1)).start()

    query_copy(0, 1, away(0, 1, -1)).wait_recv()

    def take_queries(step, carry):
        for other in range(2):
            query_copy(step + 1, other, away(step + 1, other, -1)).wait_recv()
        return carry

    repeat(chips - 1, take_queries)

    none = jnp.zeros((), jnp.bfloat16)
    for place in range(heads):
        block = inbox[pl.ds((part * heads + place) * rows, rows), :]
        own[pl.ds(place * rows, rows), :] = jnp.where(lower, block, none)
        own[pl.ds(own_rows + place * rows, rows), :] = jnp.where(lower, none, block)

    top[...] = jnp.full(top.shape, 2 * floor_value, jnp.float32)

    def score_turn(step, carry):
        right = inbox[pl.ds(step * 2 * rows, 2 * rows), :]
        raw = lax.dot_general(
            own[...], right, (((1,), (1,)), ((), ())), preferred_element_type=jnp.float32
        )
        for place in range(heads):
            for near in range(2):
                block = step * 2 + near
                bias = jnp.where(table[part * heads + place, block] >= 0, 0.0, floor_value)
                for which in range(2):
                    begin = which * own_rows + place * rows
                    at = pl.ds(begin, rows)
                    tile = (
                        raw[begin : begin + rows, near * rows : (near + 1) * rows] * score_factor
                        + bias.astype(jnp.float32)
                    )
                    scores[block, at, :] = tile
                    top[at, :] = jnp.maximum(top[at, :], tile)
        return carry

    repeat(n // 2, score_turn)

    wide = jnp.zeros((rows, LANES), jnp.float32)
    for place in range(heads):
        t_at, s_at = pl.ds(place * rows, rows), pl.ds(own_rows + place * rows, rows)
        t_high = jnp.max(top[t_at, :], axis=1, keepdims=True)
        s_high = jnp.max(top[s_at, :], axis=1, keepdims=True)
        blank = jnp.zeros((rows, LANES), jnp.float32)

        def sum_turn(block, carry):
            t_sum, s_sum, gap_sum = carry
            t_tile, s_tile = scores[block, t_at, :], scores[block, s_at, :]
            t_exp = jnp.exp2(t_tile - t_high)
            return (
                t_sum + t_exp,
                s_sum + jnp.exp2(s_tile - s_high),
                gap_sum + t_exp * (t_tile - s_tile),
            )

        t_sum, s_sum, gap_sum = [
            jnp.sum(piece, axis=1, keepdims=True)
            for piece in repeat(n, sum_turn, (blank, blank, blank))
        ]
        t_line = t_high + jnp.log2(t_sum)
        s_line = s_high + jnp.log2(s_sum)
        div_line = gap_sum / t_sum - t_line + s_line
        logs[t_at, :] = jnp.broadcast_to(t_line, (rows, LANES))
        logs[s_at, :] = jnp.broadcast_to(s_line, (rows, LANES))
        wide = jnp.where(lane == place, t_line, wide)
        wide = jnp.where(lane == heads + place, s_line, wide)
        wide = jnp.where(lane == 2 * heads + place, div_line, wide)
    stats[part] = wide.T[: stats.shape[1]]

    def stat_copy(step, target):
        return remote(
            stats.at[part], stats.at[part], stat_send.at[step], stat_recv.at[step], target
        )

    def send_stats(step, carry):
        stat_copy(step, head * parts + (part + step + 1) % parts).start()
        return carry

    repeat(parts - 1, send_stats)

    def row_turn(block, carry):
        for place in range(heads):
            t_at, s_at = pl.ds(place * rows, rows), pl.ds(own_rows + place * rows, rows)
            row_part[block, t_at, :] = jnp.exp2(scores[block, s_at, :] - logs[s_at, :]) - jnp.exp2(
                scores[block, t_at, :] - logs[t_at, :]
            )
        return carry

    repeat(n, row_turn)

    def take_stats(step, carry):
        stat_copy(step, head * parts + (part - step - 1 + parts) % parts).wait_recv()
        return carry

    repeat(parts - 1, take_stats)

    def div_turn(step, carry):
        return carry + stats[step, pl.ds(2 * heads, heads), :]

    div_sum = repeat(parts, div_turn, jnp.zeros((heads, rows), jnp.float32))
    div_sum = jnp.sum(jnp.sum(div_sum, axis=0, keepdims=True), axis=1, keepdims=True)
    out_div[...] = jnp.broadcast_to(div_sum * (math.log(2.0) / (rows * n)), out_div.shape)

    def div_copy(place, slot, target):
        return remote(out_div, in_div.at[head], back_send.at[1, place], back_recv.at[1, slot], target)

    def grad_copy(place, slot, target):
        return remote(
            out_grad.at[place], in_grad.at[head], back_send.at[0, place], back_recv.at[0, slot], target
        )

    for place in range(heads):
        target = part * heads + place

        @pl.when(target != me)
        def send_div():
            div_copy(place, head, target).start()

        @pl.when(target == me)
        def keep_div():
            keep = pltpu.make_async_copy(out_div, in_div.at[head], local_sem.at[0])
            keep.start()
            keep.wait()

    half_lower = lax.broadcasted_iota(jnp.int32, (half, LANES), 1) < HEAD_DIM
    run = heads // 2
    for turn in range(2):
        place_base = (chip + 1 + turn) % 2 * run

        def gradient_turn(step, carry):
            lines = []
            for inner in range(run):
                place = place_base + inner
                t_at = pl.ds(pl.multiple_of(place * rows, rows), rows)
                s_at = pl.ds(pl.multiple_of(own_rows + place * rows, rows), rows)
                pieces = []
                for near in range(2):
                    block = step * 2 + near
                    line = stats.at[block // heads]
                    t_line = line[pl.ds(block % heads, 1), :]
                    s_line = line[pl.ds(heads + block % heads, 1), :]
                    column_part = jnp.exp2(scores[block, s_at, :] - s_line) - jnp.exp2(
                        scores[block, t_at, :] - t_line
                    )
                    pieces.append((row_part[block, t_at, :] + column_part).astype(jnp.bfloat16))
                lines.append(jnp.concatenate(pieces, axis=1))
            return carry + jnp.dot(
                jnp.concatenate(lines, axis=0),
                inbox[pl.ds(step * 2 * rows, 2 * rows), :],
                preferred_element_type=jnp.float32,
            )

        total = repeat(n // 2, gradient_turn, jnp.zeros((run * rows, LANES), jnp.float32))
        for inner in range(run):
            place = place_base + inner
            target = part * heads + place
            upper_rows = total[inner * rows : inner * rows + half]
            lower_rows = total[inner * rows + half : (inner + 1) * rows]
            out_grad[place] = (
                jnp.where(half_lower, pltpu.roll(upper_rows, HEAD_DIM, 1), lower_rows)
                * (distill_weight * HEAD_DIM ** (-0.5))
            ).astype(jnp.bfloat16)

            @pl.when(target != me)
            def send_grad():
                grad_copy(place, head, target).start()

    @pl.when(part == me // heads)
    def keep_grad():
        keep = pltpu.make_async_copy(out_grad.at[me % heads], in_grad.at[head], local_sem.at[1])
        keep.start()
        keep.wait()

    for slot in range(heads):
        source = slot * parts + me // heads

        @pl.when(source != me)
        def take_back():
            div_copy(0, slot, source).wait_recv()
            grad_copy(0, slot, source).wait_recv()

    query_copy(0, 1, away(0, 1, 1)).wait_send()

    def drain(step, carry):
        for other in range(2):
            query_copy(step + 1, other, away(step + 1, other, 1)).wait_send()
        return carry

    repeat(chips - 1, drain)

    def drain_stats(step, carry):
        stat_copy(step, head * parts + (part + step + 1) % parts).wait_send()
        return carry

    repeat(parts - 1, drain_stats)
    for place in range(heads):
        target = part * heads + place

        @pl.when(target != me)
        def drain_back():
            div_copy(place, head, target).wait_send()
            grad_copy(place, head, target).wait_send()


def unpack(in_grad, in_div, grad_ref, div_ref):
    heads, half = in_grad.shape[:2]
    group = LANES // HEAD_DIM
    half_lower = lax.broadcasted_iota(jnp.int32, (half, LANES), 1) < HEAD_DIM
    for pair in range(heads // group):
        first = in_grad[pair * group].astype(jnp.float32)
        second = in_grad[pair * group + 1].astype(jnp.float32)
        columns = pl.ds(pair * LANES, LANES)
        grad_ref[pl.ds(0, half), columns] = jnp.where(
            half_lower, first, pltpu.roll(second, HEAD_DIM, 1)
        ).astype(jnp.bfloat16)
        grad_ref[pl.ds(half, half), columns] = jnp.where(
            half_lower, pltpu.roll(first, HEAD_DIM, 1), second
        ).astype(jnp.bfloat16)
    div_lane = lax.broadcasted_iota(jnp.int32, (1, LANES), 1)
    div_row = jnp.zeros((1, LANES), jnp.float32)
    for slot in range(heads):
        div_row = jnp.where(div_lane == slot, in_div[slot, pl.ds(0, 1), :], div_row)
    div_ref[...] = div_row[:, :heads]


def per_device(n, teacher_q, student_q, owner_table):
    rows, width = teacher_q.shape
    heads = width // HEAD_DIM
    chips = n // 2
    parts = n // heads
    stat_rows = -(-3 * heads // 8) * 8
    hbm = pl.BlockSpec(memory_space=pl.ANY)
    packed = pl.pallas_call(
        functools.partial(kernel, n),
        out_shape=(
            jax.ShapeDtypeStruct((heads, rows // 2, LANES), jnp.bfloat16),
            jax.ShapeDtypeStruct((heads, 8, LANES), jnp.float32),
        ),
        in_specs=[hbm, hbm, pl.BlockSpec(memory_space=pltpu.SMEM)],
        out_specs=(hbm, hbm),
        scratch_shapes=[
            pltpu.VMEM((rows, width), jnp.bfloat16),
            pltpu.VMEM((rows, width), jnp.bfloat16),
            pltpu.VMEM((heads, rows, LANES), jnp.bfloat16),
            pltpu.VMEM((n * rows, LANES), jnp.bfloat16),
            pltpu.VMEM((2 * heads * rows, LANES), jnp.bfloat16),
            pltpu.VMEM((n, 2 * heads * rows, rows), jnp.float32),
            pltpu.VMEM((2 * heads * rows, rows), jnp.float32),
            pltpu.VMEM((2 * heads * rows, LANES), jnp.float32),
            pltpu.VMEM((n, heads * rows, rows), jnp.float32),
            pltpu.VMEM((parts, stat_rows, rows), jnp.float32),
            pltpu.VMEM((heads, rows // 2, LANES), jnp.bfloat16),
            pltpu.VMEM((8, LANES), jnp.float32),
            pltpu.SemaphoreType.DMA((2,)),
            pltpu.SemaphoreType.DMA((chips, 2)),
            pltpu.SemaphoreType.DMA((chips, 2)),
            pltpu.SemaphoreType.DMA((parts,)),
            pltpu.SemaphoreType.DMA((parts,)),
            pltpu.SemaphoreType.DMA((2, heads)),
            pltpu.SemaphoreType.DMA((2, heads)),
        ],
        compiler_params=pltpu.CompilerParams(
            collective_id=0, has_side_effects=True, vmem_limit_bytes=60 * 1024 * 1024
        ),
        name="distill",
    )(teacher_q, student_q, owner_table)
    grad, divergence = pl.pallas_call(
        unpack,
        out_shape=(
            jax.ShapeDtypeStruct((rows, width), jnp.bfloat16),
            jax.ShapeDtypeStruct((1, heads), jnp.float32),
        ),
        in_specs=[pl.BlockSpec(memory_space=pltpu.VMEM)] * 2,
        out_specs=(pl.BlockSpec(memory_space=pltpu.VMEM),) * 2,
        name="unpack",
    )(*packed)
    return (grad, divergence.reshape(heads))


def solution(mesh):
    placed = (P("tok", "head"), P("tok", "head"), P())
    return jax.shard_map(
        functools.partial(per_device, mesh.shape["tok"]),
        mesh=mesh,
        in_specs=placed,
        out_specs=(P("tok", "head"), P("head")),
        check_vma=False,
    )
```

profile of v0, /device:TPU:0, one launch (start us, length us, event | category | flops | bytes accessed | tf_op | source)
XLA Modules:
  0.0 18.0 jit_solution(5301773437347543626)
XLA Ops:
  0.6 15.8 %distill.1 = (bf16[4,64,128]{2,1,0:T(8,128)(2,1)}, f32[4,8,128]{2,1,0:T(8,128)}) custom-call(bf16[128,256]{1,0:T(8,128)(2,1)} %teacher_hbm.1, bf16[128,256]{1,0:T(8,128)(2,1)} %student_hbm.1, s32[8,8]{1,0:T(8,128)} %table.1), custom_call_target="tpu_custom_call" | custom-call | tf_op jit(solution)/shard_map/distill/pallas_call | solution.py:346
  16.4 1.6 %unpack.1 = (bf16[128,256]{1,0:T(8,128)(2,1)}, f32[1,4]{1,0:T(1,128)}) custom-call(bf16[4,64,128]{2,1,0:T(8,128)(2,1)} %get-tuple-element.6.in_grad, f32[4,8,128]{2,1,0:T(8,128)} %get-tuple-element.7.in_div), custom_call_target="tpu_custom_call" | custom-call | tf_op jit(solution)/shard_map/unpack/pallas_call | solution.py:380
where the time goes:
time: 18.2 us; the launch traced here: 18 us
  Pallas kernels  17.4 us (96%)
  between operations  0.64 us (4%)
    pallas_call x1, Pallas kernels, per_device(): pl.pallas_call(functools.partial(kernel, n), out_shape=(jax.ShapeDtypeStr...  15.8 us
    pallas_call x1, Pallas kernels, per_device(): pl.pallas_call(unpack, out_shape=(jax.ShapeDtypeStruct((rows, width), jnp...  1.56 us

commit v1 on v0

--- a/solution.py
+++ b/solution.py
@@ -25,9 +25,9 @@
 
 
 def kernel(
-    n, teacher_hbm, student_hbm, table, in_grad, in_div,
+    n, teacher_hbm, student_hbm, table_hbm, in_grad, in_div,
     teacher, student, outbox, inbox, own, scores, top, logs, row_part, stats,
-    out_grad, out_div, local_sem, send_sem, recv_sem, stat_send, stat_recv, back_send, back_recv,
+    out_grad, out_div, local_sem, send_sem, recv_sem, stat_send, stat_recv, back_send, back_recv, table, tab_sem,
 ):
     rows, width = teacher_hbm.shape
     pairs = width // LANES
@@ -66,6 +66,8 @@
     ]
     for load in loads:
         load.start()
+    tload = pltpu.make_async_copy(table_hbm, table, tab_sem)
+    tload.start()
 
     def greet(d, carry):
         pl.semaphore_signal(barrier, inc=1, device_id=spot((me + d + 1) % n), device_id_type=MESH)
@@ -125,6 +127,7 @@
         own[pl.ds(place * rows, rows), :] = jnp.where(lower, block, none)
         own[pl.ds(own_rows + place * rows, rows), :] = jnp.where(lower, none, block)
 
+    tload.wait()
     top[...] = jnp.full(top.shape, 2 * floor_value, jnp.float32)
 
     def score_turn(step, carry):
@@ -346,11 +349,11 @@
     packed = pl.pallas_call(
         functools.partial(kernel, n),
         out_shape=(
-            jax.ShapeDtypeStruct((heads, rows // 2, LANES), jnp.bfloat16),
-            jax.ShapeDtypeStruct((heads, 8, LANES), jnp.float32),
+            pltpu.VMEM((heads, rows // 2, LANES), jnp.bfloat16),
+            pltpu.VMEM((heads, 8, LANES), jnp.float32),
         ),
-        in_specs=[hbm, hbm, pl.BlockSpec(memory_space=pltpu.SMEM)],
-        out_specs=(hbm, hbm),
+        in_specs=[pl.BlockSpec(memory_space=pltpu.HBM)] * 3,
+        out_specs=(pl.BlockSpec(memory_space=pl.ANY),) * 2,
         scratch_shapes=[
             pltpu.VMEM((rows, width), jnp.bfloat16),
             pltpu.VMEM((rows, width), jnp.bfloat16),
@@ -371,12 +374,14 @@
             pltpu.SemaphoreType.DMA((parts,)),
             pltpu.SemaphoreType.DMA((2, heads)),
             pltpu.SemaphoreType.DMA((2, heads)),
+            pltpu.SMEM((n, n), jnp.int32),
+            pltpu.SemaphoreType.DMA,
         ],
         compiler_params=pltpu.CompilerParams(
             collective_id=0, has_side_effects=True, vmem_limit_bytes=60 * 1024 * 1024
         ),
         name="distill",
-    )(teacher_q, student_q, owner_table)
+    )(*[pltpu.with_memory_space_constraint(x, pltpu.HBM) for x in (teacher_q, student_q, owner_table)])
     grad, divergence = pl.pallas_call(
         unpack,
         out_shape=(
@@ -385,6 +390,7 @@
         ),
         in_specs=[pl.BlockSpec(memory_space=pltpu.VMEM)] * 2,
         out_specs=(pl.BlockSpec(memory_space=pltpu.VMEM),) * 2,
+        compiler_params=pltpu.CompilerParams(vmem_limit_bytes=4 * 1024 * 1024),
         name="unpack",
     )(*packed)
     return (grad, divergence.reshape(heads))

time: 18.2 us -> 16.6 us (0.912)
  Pallas kernels: 17.4 us -> 15.7 us
    pallas_call x1, Pallas kernels: 1.56 us -> 0.72 us  [per_device(): pl.pallas_call(unpack, out_shape=(jax.ShapeDtypeStruct((rows, width), jnp...]
    pallas_call x1, Pallas kernels: 15.8 us -> 15 us  [per_device(): pl.pallas_call(functools.partial(kernel, n), out_shape=(pltpu.VMEM((heads...]
where the time goes in v1:
time: 16.6 us; the launch traced here: 16.4 us
  Pallas kernels  15.7 us (95%)
  between operations  0.64 us (4%)
    pallas_call x1, Pallas kernels, per_device(): pl.pallas_call(functools.partial(kernel, n), out_shape=(pltpu.VMEM((heads...  15 us
    pallas_call x1, Pallas kernels, per_device(): pl.pallas_call(unpack, out_shape=(jax.ShapeDtypeStruct((rows, width), jnp...  0.72 us

profile of v1, /device:TPU:0, one launch (start us, length us, event | category | flops | bytes accessed | tf_op | source)
XLA Modules:
  0.0 16.4 jit_solution(7459260886892692195)
XLA Ops:
  0.6 15.0 %distill.1 = (bf16[4,64,128]{2,1,0:T(8,128)(2,1)S(1)}, f32[4,8,128]{2,1,0:T(8,128)S(1)}) custom-call(bf16[128,256]{1,0:T(8,128)(2,1)} %teacher_hbm.1, bf16[128,256]{1,0:T(8,128)(2,1)} %student_hbm.1, s32[8,8]{1,0:T(8,128)} %table_hbm.1), custom_call_target="tpu_custom_call" | custom-call | tf_op jit(solution)/shard_map/distill/pallas_call | solution.py:349
  15.7 0.7 %unpack.1 = (bf16[128,256]{1,0:T(8,128)(2,1)}, f32[1,4]{1,0:T(1,128)}) custom-call(bf16[4,64,128]{2,1,0:T(8,128)(2,1)S(1)} %get-tuple-element.6.in_grad, f32[4,8,128]{2,1,0:T(8,128)S(1)} %get-tuple-element.7.in_div), custom_call_target="tpu_custom_call" | custom-call | tf_op jit(solution)/shard_map/unpack/pallas_call | solution.py:385

commit v2 on v1

v2 whole, which is shorter than its diff:
```python
import functools
import math

import jax
import jax.numpy as jnp
from jax import lax
from jax.experimental import pallas as pl
from jax.experimental.pallas import tpu as pltpu
from jax.sharding import PartitionSpec as P

HEAD_DIM = 64
LANES = 128
NOTE_ROWS = 16
KEEP_BYTES = 16 * 1024 * 1024
floor_value = -3e38
distill_weight = 32.0
score_factor = HEAD_DIM ** (-0.5) * math.log2(math.e)
MESH = pl.DeviceIdType.MESH


def repeat(count, body, init=None):
    if count <= 16:
        for step in range(count):
            init = body(step, init)
        return init
    return lax.fori_loop(0, count, body, init)


def kernel(
    n, most, keep, teacher_hbm, student_hbm, table_hbm, in_grad,
    teacher, student, outbox, inbox, left, turned, table, before, following,
    edge_row, edge_col, edge_back, edge_tag, tags, stats, weights, exps, gaps,
    running, diagonal, out_grad, load_sem, table_sem, send_sem, recv_sem, back_send, back_recv,
):
    rows, width = teacher_hbm.shape
    pairs = width // LANES
    heads = width // HEAD_DIM
    group = LANES // HEAD_DIM
    parts = n // heads
    chips = n // 2
    side = math.isqrt(chips)
    side = side if side * side == chips else 1
    span = chips // side
    me = lax.axis_index("tok")
    head_at = lax.axis_index("head")
    chip, core = me // 2, me % 2
    head = me // parts
    is_worker = me % parts == 0

    def place(step):
        shift, flip = step // 2, step % 2
        high = (chip // span + shift // span) % side
        low = (chip % span + shift % span) % span
        return (high * span + low) * 2 + (core + flip) % 2

    def place_in(worker):
        worker_chip = worker // 2
        high = (chip // span - worker_chip // span + side) % side
        low = (chip % span - worker_chip % span + span) % span
        return (high * span + low) * 2 + (core - worker % 2 + 2) % 2

    def remote(src, dst, send, recv, target):
        return pltpu.make_async_remote_copy(
            src_ref=src, dst_ref=dst, send_sem=send, recv_sem=recv,
            device_id=(head_at, target), device_id_type=MESH,
        )

    barrier = pltpu.get_barrier_semaphore()
    loads = [
        pltpu.make_async_copy(teacher_hbm, teacher, load_sem.at[0]),
        pltpu.make_async_copy(student_hbm, student, load_sem.at[1]),
    ]
    for load in loads:
        load.start()
    table_load = pltpu.make_async_copy(table_hbm, table, table_sem)
    table_load.start()

    def greet(target):
        pl.semaphore_signal(barrier, inc=1, device_id=(head_at, target), device_id_type=MESH)

    @pl.when(is_worker)
    def greet_all():
        def greet_one(step, carry):
            greet(place(n - 1 - step))
            return carry

        repeat(n - 1, greet_one)

    @pl.when(jnp.logical_not(is_worker))
    def greet_workers():
        for step in range(heads):
            greet((head + heads - 1 - step) % heads * parts)

    for load in loads:
        load.wait()
    lane = lax.broadcasted_iota(jnp.int32, (rows, LANES), 1)
    lower = lane < HEAD_DIM
    for pair in range(pairs):
        columns = pl.ds(pair * LANES, LANES)
        t_pair = teacher[:, columns].astype(jnp.float32)
        s_pair = student[:, columns].astype(jnp.float32)
        outbox[pair * group] = jnp.where(lower, t_pair, pltpu.roll(s_pair, HEAD_DIM, 1)).astype(
            jnp.bfloat16
        )
        outbox[pair * group + 1] = jnp.where(
            lower, pltpu.roll(t_pair, HEAD_DIM, 1), s_pair
        ).astype(jnp.bfloat16)

    def query_copy(to_head, slot):
        return remote(
            outbox.at[to_head], inbox.at[slot], send_sem.at[to_head], recv_sem.at[slot],
            to_head * parts,
        )

    def send_queries():
        for step in range(heads - 1, 0, -1):
            to_head = (head + step) % heads
            query_copy(to_head, place_in(to_head * parts)).start()

    def drain_queries():
        for step in range(heads - 1, 0, -1):
            query_copy((head + step) % heads, 0).wait_send()

    def grad_copy(slot, target):
        return remote(
            out_grad.at[slot], in_grad.at[head], back_send.at[slot], back_recv.at[head], target
        )

    def take_grads(own):
        for step in range(heads):
            from_head = (head + step) % heads
            if step == 0 and own:
                continue
            remote(
                out_grad.at[0], in_grad.at[from_head], back_send.at[0], back_recv.at[from_head],
                from_head * parts,
            ).wait_recv()

    @pl.when(jnp.logical_not(is_worker))
    def serve():
        pl.semaphore_wait(barrier, heads)
        send_queries()
        query_copy(head, place_in(head * parts)).start()
        drain_queries()
        query_copy(head, 0).wait_send()
        table_load.wait()
        take_grads(False)

    @pl.when(is_worker)
    def work():
        inbox[0] = outbox[head]
        pl.semaphore_wait(barrier, n - 1)
        send_queries()
        table_load.wait()
        codes = n * n

        def count_row(rank, count):
            row = n - 1 - rank
            row_at = place(row)

            def count_cell(col, count):
                inside = jnp.logical_and(table[row_at, place(col)] >= 0, col != row)
                before[rank * n + col] = count
                return count + jnp.where(inside, 1, 0)

            return repeat(n, count_cell, count)

        before[codes] = repeat(n, count_row, jnp.int32(0))
        following[codes] = jnp.int32(codes)
        following[codes + 1] = jnp.int32(codes)

        def link_row(step, after):
            rank = n - 1 - step
            row = step
            row_at = place(row)

            def link_cell(back, after):
                col = n - 1 - back
                inside = jnp.logical_and(table[row_at, place(col)] >= 0, col != row)
                after = jnp.where(inside, rank * n + col, after)
                following[rank * n + col] = after
                return after

            return repeat(n, link_cell, after)

        repeat(n, link_row, jnp.int32(codes))

        def list_edge(edge, code):
            code = following[code + 1]
            held = jnp.minimum(code, codes - 1)
            row, col = n - 1 - held // n, held % n
            edge_row[edge] = row
            edge_col[edge] = col
            edge_back[edge] = jnp.minimum(before[(n - 1 - col) * n + row], most - 1)
            tag = jnp.where(code < codes, row, -1)
            edge_tag[edge] = tag
            tags[pl.ds(edge, 1), :] = jnp.full((1, LANES), tag, jnp.int32)
            return code

        repeat(most, list_edge, jnp.int32(-1))

        def tag_diagonal(slot, carry):
            tags[pl.ds(most + slot, 1), :] = jnp.full((1, LANES), slot, jnp.int32)
            return carry

        repeat(n, tag_diagonal)

        def scores(col, row):
            raw = lax.dot_general(
                left[col], inbox[row], (((1,), (1,)), ((), ())),
                preferred_element_type=jnp.float32,
            )
            return raw[:rows], raw[rows:]

        def measure(entry, col, row):
            t_raw, s_raw = scores(col, row)
            t_top = jnp.max(t_raw, axis=0, keepdims=True)
            s_top = jnp.max(s_raw, axis=0, keepdims=True)
            t_exp = jnp.exp2((t_raw - t_top) * score_factor)
            s_exp = jnp.exp2((s_raw - s_top) * score_factor)
            at = pl.ds(entry, 1)
            stats[0, at, :] = t_top
            stats[1, at, :] = s_top
            stats[2, at, :] = jnp.sum(t_exp, axis=0, keepdims=True)
            stats[3, at, :] = jnp.sum(s_exp, axis=0, keepdims=True)
            stats[4, at, :] = jnp.sum(t_exp * (t_raw - s_raw), axis=0, keepdims=True)
            if keep:
                exps[entry, 0] = t_exp
                exps[entry, 1] = s_exp

        none = jnp.zeros((), jnp.bfloat16)

        def take_block(slot, carry):
            @pl.when(slot > 0)
            def wait_block():
                remote(
                    outbox.at[0], inbox.at[slot], send_sem.at[0], recv_sem.at[slot], place(slot)
                ).wait_recv()

            block = inbox[slot]
            left[slot, pl.ds(0, rows), :] = jnp.where(lower, block, none)
            left[slot, pl.ds(rows, rows), :] = jnp.where(lower, none, block)
            turned[slot] = block.T[HEAD_DIM:]
            measure(most + slot, slot, slot)
            return carry

        repeat(n, take_block)

        def measure_edge(edge, carry):
            measure(edge, edge_col[edge], edge_row[edge])
            return carry

        repeat(most, measure_edge)

        weights[...] = jnp.zeros(weights.shape, jnp.float32)

        def combine(slot, total):
            mine = tags[...] == slot
            tops, sums = [], []
            for which in range(2):
                peak = stats[which]
                top = jnp.max(jnp.where(mine, peak, floor_value), axis=0, keepdims=True)
                part = jnp.exp2(jnp.where(mine, (peak - top) * score_factor, floor_value))
                amount = jnp.sum(part * stats[2 + which], axis=0, keepdims=True)
                inverse = 1.0 / amount
                weights[which] = jnp.where(mine, part * inverse, weights[which])
                if which == 0:
                    cross = jnp.sum(part * stats[4], axis=0, keepdims=True) * inverse
                tops.append(top)
                sums.append(amount)
            return (
                total
                + (cross - tops[0] + tops[1]) * score_factor
                - jnp.log2(sums[0])
                + jnp.log2(sums[1])
            )

        total = repeat(n, combine, jnp.zeros((1, LANES), jnp.float32))
        total = jnp.sum(total, axis=1, keepdims=True) * (math.log(2.0) / (rows * n))
        first = total.astype(jnp.bfloat16).astype(jnp.float32)
        second = (total - first).astype(jnp.bfloat16).astype(jnp.float32)
        note_row = lax.broadcasted_iota(jnp.int32, (NOTE_ROWS, LANES), 0)
        note = jnp.where(
            note_row == 0,
            first,
            jnp.where(
                note_row == 1, second, jnp.where(note_row == 2, total - first - second, 0.0)
            ),
        ).astype(jnp.bfloat16)

        def gap_of(entry, col, row):
            at = pl.ds(entry, 1)
            if keep:
                t_exp, s_exp = exps[entry, 0], exps[entry, 1]
            else:
                t_raw, s_raw = scores(col, row)
                t_exp = jnp.exp2((t_raw - stats[0, at, :]) * score_factor)
                s_exp = jnp.exp2((s_raw - stats[1, at, :]) * score_factor)
            gaps[entry] = (s_exp * weights[1, at, :] - t_exp * weights[0, at, :]).astype(
                jnp.bfloat16
            )

        def gap_edge(edge, carry):
            gap_of(edge, edge_col[edge], edge_row[edge])
            return carry

        def gap_diagonal(slot, carry):
            gap_of(most + slot, slot, slot)
            return carry

        repeat(most, gap_edge)
        repeat(n, gap_diagonal)

        def product(col, entry, back):
            query = turned[col]
            return jnp.dot(
                query, gaps[entry], preferred_element_type=jnp.float32
            ) + lax.dot_general(
                query, gaps[back], (((1,), (1,)), ((), ())), preferred_element_type=jnp.float32
            )

        def add_edge(edge, carry):
            line, last = carry
            tag = edge_tag[edge]
            fresh = product(edge_col[edge], edge, edge_back[edge])
            line = jnp.where(tag == last, line, 0.0) + fresh
            running[edge] = line
            return line, tag

        repeat(most, add_edge, (jnp.zeros((HEAD_DIM, rows), jnp.float32), jnp.int32(-1)))

        def finish(step, carry):
            slot = n - 1 - step
            start, stop = before[step * n], before[(step + 1) * n]
            line = product(slot, most + slot, most + slot) + jnp.where(
                stop > start, running[jnp.clip(stop - 1, 0, most - 1)], 0.0
            )
            out_grad[slot, pl.ds(0, HEAD_DIM), :] = (
                line * (distill_weight * HEAD_DIM ** (-0.5))
            ).astype(jnp.bfloat16)
            out_grad[slot, pl.ds(HEAD_DIM, NOTE_ROWS), :] = note

            @pl.when(slot > 0)
            def send_grad():
                grad_copy(slot, place(slot)).start()

            return carry

        repeat(n, finish)
        in_grad[head] = out_grad[0]
        drain_queries()
        take_grads(True)

        def drain_grads(step, carry):
            grad_copy(step + 1, place(step + 1)).wait_send()
            return carry

        repeat(n - 1, drain_grads)


def unpack(in_grad, grad_ref, div_ref):
    heads = in_grad.shape[0]
    group = LANES // HEAD_DIM
    for pair in range(heads // group):
        both = jnp.concatenate(
            [in_grad[pair * group + inner, pl.ds(0, HEAD_DIM), :] for inner in range(group)], axis=0
        )
        grad_ref[:, pl.ds(pair * LANES, LANES)] = both.T
    div_lane = lax.broadcasted_iota(jnp.int32, (1, LANES), 1)
    div_row = jnp.zeros((1, LANES), jnp.float32)
    for slot in range(heads):
        note = in_grad[slot, pl.ds(HEAD_DIM, NOTE_ROWS), :].astype(jnp.float32)
        div_row = jnp.where(div_lane == slot, jnp.sum(note, axis=0, keepdims=True), div_row)
    div_ref[...] = div_row[:, :heads]


def per_device(n, teacher_q, student_q, owner_table):
    rows, width = teacher_q.shape
    heads = width // HEAD_DIM
    owned = n // heads
    most = 2 * (n * owned - n)
    entries = most + n
    keep = entries * 2 * rows * rows * 4 <= KEEP_BYTES
    hbm = pl.BlockSpec(memory_space=pl.ANY)
    message = HEAD_DIM + NOTE_ROWS
    packed = pl.pallas_call(
        functools.partial(kernel, n, most, keep),
        out_shape=pltpu.VMEM((heads, message, rows), jnp.bfloat16),
        in_specs=[hbm, hbm, hbm],
        out_specs=pl.BlockSpec(memory_space=pltpu.VMEM),
        scratch_shapes=[
            pltpu.VMEM((rows, width), jnp.bfloat16),
            pltpu.VMEM((rows, width), jnp.bfloat16),
            pltpu.VMEM((heads, rows, LANES), jnp.bfloat16),
            pltpu.VMEM((n, rows, LANES), jnp.bfloat16),
            pltpu.VMEM((n, 2 * rows, LANES), jnp.bfloat16),
            pltpu.VMEM((n, HEAD_DIM, rows), jnp.bfloat16),
            pltpu.SMEM((n, n), jnp.int32),
            pltpu.SMEM((n * n + 1,), jnp.int32),
            pltpu.SMEM((n * n + 2,), jnp.int32),
            pltpu.SMEM((most,), jnp.int32),
            pltpu.SMEM((most,), jnp.int32),
            pltpu.SMEM((most,), jnp.int32),
            pltpu.SMEM((most,), jnp.int32),
            pltpu.VMEM((entries, rows), jnp.int32),
            pltpu.VMEM((5, entries, rows), jnp.float32),
            pltpu.VMEM((2, entries, rows), jnp.float32),
            pltpu.VMEM((entries if keep else 1, 2, rows, rows), jnp.float32),
            pltpu.VMEM((entries, rows, rows), jnp.bfloat16),
            pltpu.VMEM((most, HEAD_DIM, rows), jnp.float32),
            pltpu.VMEM((8, LANES), jnp.float32),
            pltpu.VMEM((n, message, rows), jnp.bfloat16),
            pltpu.SemaphoreType.DMA((2,)),
            pltpu.SemaphoreType.DMA,
            pltpu.SemaphoreType.DMA((heads,)),
            pltpu.SemaphoreType.DMA((n,)),
            pltpu.SemaphoreType.DMA((n,)),
            pltpu.SemaphoreType.DMA((heads,)),
        ],
        compiler_params=pltpu.CompilerParams(
            collective_id=0, has_side_effects=True, vmem_limit_bytes=60 * 1024 * 1024
        ),
        name="distill",
    )(*[pltpu.with_memory_space_constraint(x, pltpu.HBM) for x in (teacher_q, student_q, owner_table)])
    grad, divergence = pl.pallas_call(
        unpack,
        out_shape=(
            jax.ShapeDtypeStruct((rows, width), jnp.bfloat16),
            jax.ShapeDtypeStruct((1, heads), jnp.float32),
        ),
        in_specs=[pl.BlockSpec(memory_space=pltpu.VMEM)],
        out_specs=(pl.BlockSpec(memory_space=pltpu.VMEM),) * 2,
        compiler_params=pltpu.CompilerParams(vmem_limit_bytes=4 * 1024 * 1024),
        name="unpack",
    )(packed)
    return (grad, divergence.reshape(heads))


def solution(mesh):
    placed = (P("tok", "head"), P("tok", "head"), P())
    return jax.shard_map(
        functools.partial(per_device, mesh.shape["tok"]),
        mesh=mesh,
        in_specs=placed,
        out_specs=(P("tok", "head"), P("head")),
        check_vma=False,
    )
```

time: 16.6 us -> 15.7 us (0.946)
  Pallas kernels: 15.7 us -> 14.9 us
    pallas_call x1, Pallas kernels: 15 us -> 14.2 us  [per_device(): pl.pallas_call(functools.partial(kernel, n, most, keep), out_shape=pltpu....]
where the time goes in v2:
time: 15.7 us; the launch traced here: 15.6 us
  Pallas kernels  14.9 us (95%)
  between operations  0.64 us (4%)
    pallas_call x1, Pallas kernels, per_device(): pl.pallas_call(functools.partial(kernel, n, most, keep), out_shape=pltpu....  14.2 us
    pallas_call x1, Pallas kernels, per_device(): pl.pallas_call(unpack, out_shape=(jax.ShapeDtypeStruct((rows, width), jnp...  0.7 us

profile of v2, /device:TPU:0, one launch (start us, length us, event | category | flops | bytes accessed | tf_op | source)
XLA Modules:
  0.0 15.6 jit_solution(15047368934980160726)
XLA Ops:
  0.6 14.2 %distill.1.in_grad = bf16[4,80,128]{2,1,0:T(8,128)(2,1)S(1)} custom-call(bf16[128,256]{1,0:T(8,128)(2,1)} %teacher_hbm.1, bf16[128,256]{1,0:T(8,128)(2,1)} %student_hbm.1, s32[8,8]{1,0:T(8,128)} %table_hbm.1), custom_call_target="tpu_custom_call" | custom-call | tf_op jit(solution)/shard_map/distill/pallas_call | solution.py:386
  14.9 0.7 %unpack.1 = (bf16[128,256]{1,0:T(8,128)(2,1)}, f32[1,4]{1,0:T(1,128)}) custom-call(bf16[4,80,128]{2,1,0:T(8,128)(2,1)S(1)} %distill.1.in_grad), custom_call_target="tpu_custom_call" | custom-call | tf_op jit(solution)/shard_map/unpack/pallas_call | solution.py:425

commit v3 on v2

--- a/solution.py
+++ b/solution.py
@@ -28,9 +28,9 @@
 
 def kernel(
     n, most, keep, teacher_hbm, student_hbm, table_hbm, in_grad,
-    teacher, student, outbox, inbox, left, turned, table, before, following,
-    edge_row, edge_col, edge_back, edge_tag, tags, stats, weights, exps, gaps,
-    running, diagonal, out_grad, load_sem, table_sem, send_sem, recv_sem, back_send, back_recv,
+    teacher, student, outbox, inbox, turned, table, following, edge_of,
+    edge_row, edge_col, edge_tag, stats, peaks, inverses, weights, exps, shares,
+    out_grad, load_sem, table_sem, send_sem, recv_sem, back_send, back_recv,
 ):
     rows, width = teacher_hbm.shape
     pairs = width // LANES
@@ -153,62 +153,72 @@
         send_queries()
         table_load.wait()
         codes = n * n
-
-        def count_row(rank, count):
-            row = n - 1 - rank
+        blank = most
+        own = most + 1
+
+        def count_row(row, count):
             row_at = place(row)
 
             def count_cell(col, count):
-                inside = jnp.logical_and(table[row_at, place(col)] >= 0, col != row)
-                before[rank * n + col] = count
+                inside = table[row_at, place(col)] >= 0
+                edge = jnp.minimum(2 * count, most - 2)
+                edge_of[row * n + col] = jnp.where(inside, edge, blank)
+                edge_of[col * n + row] = jnp.where(inside, edge + 1, blank)
                 return count + jnp.where(inside, 1, 0)
 
-            return repeat(n, count_cell, count)
-
-        before[codes] = repeat(n, count_row, jnp.int32(0))
+            return lower_cells(row, count_cell, count)
+
+        def lower_cells(row, body, init):
+            if isinstance(row, int):
+                for col in range(row):
+                    init = body(col, init)
+                return init
+            return lax.fori_loop(0, row, body, init)
+
+        repeat(n, count_row, jnp.int32(0))
         following[codes] = jnp.int32(codes)
         following[codes + 1] = jnp.int32(codes)
 
         def link_row(step, after):
-            rank = n - 1 - step
-            row = step
+            row = n - 1 - step
             row_at = place(row)
+            following[row * n + row] = after
 
             def link_cell(back, after):
-                col = n - 1 - back
-                inside = jnp.logical_and(table[row_at, place(col)] >= 0, col != row)
-                after = jnp.where(inside, rank * n + col, after)
-                following[rank * n + col] = after
+                col = row - 1 - back
+                code = row * n + col
+                after = jnp.where(table[row_at, place(col)] >= 0, code, after)
+                following[code] = after
                 return after
 
-            return repeat(n, link_cell, after)
+            return lower_cells(row, link_cell, after)
 
         repeat(n, link_row, jnp.int32(codes))
 
-        def list_edge(edge, code):
-            code = following[code + 1]
+        def list_pair(pair, code):
+            code = following[code]
             held = jnp.minimum(code, codes - 1)
-            row, col = n - 1 - held // n, held % n
-            edge_row[edge] = row
-            edge_col[edge] = col
-            edge_back[edge] = jnp.minimum(before[(n - 1 - col) * n + row], most - 1)
-            tag = jnp.where(code < codes, row, -1)
-            edge_tag[edge] = tag
-            tags[pl.ds(edge, 1), :] = jnp.full((1, LANES), tag, jnp.int32)
-            return code
-
-        repeat(most, list_edge, jnp.int32(-1))
-
-        def tag_diagonal(slot, carry):
-            tags[pl.ds(most + slot, 1), :] = jnp.full((1, LANES), slot, jnp.int32)
-            return carry
-
-        repeat(n, tag_diagonal)
+            high, low = held // n, held % n
+            edge_row[2 * pair] = high
+            edge_col[2 * pair] = low
+            edge_tag[2 * pair] = jnp.where(code < codes, high, -1)
+            edge_row[2 * pair + 1] = low
+            edge_col[2 * pair + 1] = high
+            edge_tag[2 * pair + 1] = jnp.where(code < codes, low, -1)
+            return code + 1
+
+        repeat(most // 2, list_pair, jnp.int32(0))
+        shares[blank] = jnp.zeros((HEAD_DIM, rows), jnp.float32)
+
+        none = jnp.zeros((), jnp.bfloat16)
 
         def scores(col, row):
+            block = inbox[col]
+            masked = jnp.concatenate(
+                [jnp.where(lower, block, none), jnp.where(lower, none, block)], axis=0
+            )
             raw = lax.dot_general(
-                left[col], inbox[row], (((1,), (1,)), ((), ())),
-                preferred_element_type=jnp.float32,
+                masked, inbox[row], (((1,), (1,)), ((), ())), preferred_element_type=jnp.float32
             )
             return raw[:rows], raw[rows:]
 
@@ -228,23 +238,23 @@
                 exps[entry, 0] = t_exp
                 exps[entry, 1] = s_exp
 
-        none = jnp.zeros((), jnp.bfloat16)
-
-        def take_block(slot, carry):
-            @pl.when(slot > 0)
-            def wait_block():
-                remote(
-                    outbox.at[0], inbox.at[slot], send_sem.at[0], recv_sem.at[slot], place(slot)
-                ).wait_recv()
-
-            block = inbox[slot]
-            left[slot, pl.ds(0, rows), :] = jnp.where(lower, block, none)
-            left[slot, pl.ds(rows, rows), :] = jnp.where(lower, none, block)
-            turned[slot] = block.T[HEAD_DIM:]
-            measure(most + slot, slot, slot)
-            return carry
-
-        repeat(n, take_block)
+        def take_chip(shift, carry):
+            for inner in range(2):
+                slot = 2 * shift + inner
+
+                @pl.when(slot > 0)
+                def wait_block():
+                    remote(
+                        outbox.at[0], inbox.at[slot], send_sem.at[0], recv_sem.at[slot], place(slot)
+                    ).wait_recv()
+
+            for inner in range(2):
+                slot = 2 * shift + inner
+                turned[slot] = inbox[slot].T[HEAD_DIM:]
+                measure(own + slot, slot, slot)
+            return carry
+
+        repeat(chips, take_chip)
 
         def measure_edge(edge, carry):
             measure(edge, edge_col[edge], edge_row[edge])
@@ -252,31 +262,72 @@
 
         repeat(most, measure_edge)
 
-        weights[...] = jnp.zeros(weights.shape, jnp.float32)
-
-        def combine(slot, total):
-            mine = tags[...] == slot
-            tops, sums = [], []
+        every = pl.ds(own, n)
+        slot_row = lax.broadcasted_iota(jnp.int32, (n, rows), 0)
+
+        def raise_peaks(edge, carry):
+            mine = slot_row == edge_tag[edge]
+            at = pl.ds(edge, 1)
+            return tuple(
+                jnp.maximum(peak, jnp.where(mine, stats[which, at, :], floor_value))
+                for which, peak in enumerate(carry)
+            )
+
+        tops = repeat(most, raise_peaks, (stats[0, every, :], stats[1, every, :]))
+        for which in range(2):
+            peaks[which] = tops[which]
+
+        def scaled(which, at):
+            return [stats[2 + which, at, :]] + ([stats[4, at, :]] if which == 0 else [])
+
+        parts_own = [
+            jnp.exp2((stats[which, every, :] - tops[which]) * score_factor) for which in range(2)
+        ]
+        sums = tuple(
+            parts_own[which] * amount for which in range(2) for amount in scaled(which, every)
+        )
+
+        def add_edge(edge, carry):
+            tag = edge_tag[edge]
+            mine = slot_row == tag
+            at = pl.ds(edge, 1)
+            fresh = []
             for which in range(2):
-                peak = stats[which]
-                top = jnp.max(jnp.where(mine, peak, floor_value), axis=0, keepdims=True)
-                part = jnp.exp2(jnp.where(mine, (peak - top) * score_factor, floor_value))
-                amount = jnp.sum(part * stats[2 + which], axis=0, keepdims=True)
-                inverse = 1.0 / amount
-                weights[which] = jnp.where(mine, part * inverse, weights[which])
-                if which == 0:
-                    cross = jnp.sum(part * stats[4], axis=0, keepdims=True) * inverse
-                tops.append(top)
-                sums.append(amount)
-            return (
-                total
-                + (cross - tops[0] + tops[1]) * score_factor
-                - jnp.log2(sums[0])
-                + jnp.log2(sums[1])
+                peak = peaks[which, pl.ds(jnp.maximum(tag, 0), 1), :]
+                part = jnp.exp2(jnp.minimum((stats[which, at, :] - peak) * score_factor, 0.0))
+                weights[which, at, :] = part
+                fresh += [part * amount for amount in scaled(which, at)]
+            return tuple(
+                total + jnp.where(mine, piece, 0.0)
+                for total, piece in zip(carry, fresh, strict=True)
             )
 
-        total = repeat(n, combine, jnp.zeros((1, LANES), jnp.float32))
-        total = jnp.sum(total, axis=1, keepdims=True) * (math.log(2.0) / (rows * n))
+        t_sum, cross, s_sum = repeat(most, add_edge, sums)
+        t_inverse, s_inverse = 1.0 / t_sum, 1.0 / s_sum
+        inverses[0] = t_inverse
+        inverses[1] = s_inverse
+        weights[0, every, :] = parts_own[0] * t_inverse
+        weights[1, every, :] = parts_own[1] * s_inverse
+
+        def weigh_edge(edge, carry):
+            tag = edge_tag[edge]
+            at, mine_at = pl.ds(edge, 1), pl.ds(jnp.maximum(tag, 0), 1)
+            valid = jnp.where(tag >= 0, 1.0, 0.0)
+            for which in range(2):
+                weights[which, at, :] = weights[which, at, :] * (
+                    inverses[which, mine_at, :] * valid
+                )
+            return carry
+
+        repeat(most, weigh_edge)
+        total = (
+            (cross * t_inverse - tops[0] + tops[1]) * score_factor
+            - jnp.log2(t_sum)
+            + jnp.log2(s_sum)
+        )
+        total = jnp.sum(jnp.sum(total, axis=0, keepdims=True), axis=1, keepdims=True) * (
+            math.log(2.0) / (rows * n)
+        )
         first = total.astype(jnp.bfloat16).astype(jnp.float32)
         second = (total - first).astype(jnp.bfloat16).astype(jnp.float32)
         note_row = lax.broadcasted_iota(jnp.int32, (NOTE_ROWS, LANES), 0)
@@ -296,45 +347,36 @@
                 t_raw, s_raw = scores(col, row)
                 t_exp = jnp.exp2((t_raw - stats[0, at, :]) * score_factor)
                 s_exp = jnp.exp2((s_raw - stats[1, at, :]) * score_factor)
-            gaps[entry] = (s_exp * weights[1, at, :] - t_exp * weights[0, at, :]).astype(
-                jnp.bfloat16
+            return (s_exp * weights[1, at, :] - t_exp * weights[0, at, :]).astype(jnp.bfloat16)
+
+        def product(query, gap, back):
+            return jnp.dot(query, gap, preferred_element_type=jnp.float32) + lax.dot_general(
+                query, back, (((1,), (1,)), ((), ())), preferred_element_type=jnp.float32
             )
 
-        def gap_edge(edge, carry):
-            gap_of(edge, edge_col[edge], edge_row[edge])
-            return carry
-
-        def gap_diagonal(slot, carry):
-            gap_of(most + slot, slot, slot)
-            return carry
-
-        repeat(most, gap_edge)
-        repeat(n, gap_diagonal)
-
-        def product(col, entry, back):
-            query = turned[col]
-            return jnp.dot(
-                query, gaps[entry], preferred_element_type=jnp.float32
-            ) + lax.dot_general(
-                query, gaps[back], (((1,), (1,)), ((), ())), preferred_element_type=jnp.float32
-            )
-
-        def add_edge(edge, carry):
-            line, last = carry
-            tag = edge_tag[edge]
-            fresh = product(edge_col[edge], edge, edge_back[edge])
-            line = jnp.where(tag == last, line, 0.0) + fresh
-            running[edge] = line
-            return line, tag
-
-        repeat(most, add_edge, (jnp.zeros((HEAD_DIM, rows), jnp.float32), jnp.int32(-1)))
+        def share_pair(pair, carry):
+            high, low = edge_row[2 * pair], edge_col[2 * pair]
+            gap = gap_of(2 * pair, low, high)
+            back = gap_of(2 * pair + 1, high, low)
+            shares[2 * pair] = product(turned[low], gap, back)
+            shares[2 * pair + 1] = product(turned[high], back, gap)
+            return carry
+
+        def share_own(slot, carry):
+            gap = gap_of(own + slot, slot, slot)
+            shares[own + slot] = product(turned[slot], gap, gap)
+            return carry
+
+        repeat(n, share_own)
+        repeat(most // 2, share_pair)
 
         def finish(step, carry):
             slot = n - 1 - step
-            start, stop = before[step * n], before[(step + 1) * n]
-            line = product(slot, most + slot, most + slot) + jnp.where(
-                stop > start, running[jnp.clip(stop - 1, 0, most - 1)], 0.0
-            )
+
+            def add_share(turn, line):
+                return line + shares[edge_of[slot * n + (slot + turn + 1) % n]]
+
+            line = repeat(n - 1, add_share, shares[own + slot])
             out_grad[slot, pl.ds(0, HEAD_DIM), :] = (
                 line * (distill_weight * HEAD_DIM ** (-0.5))
             ).astype(jnp.bfloat16)
@@ -379,7 +421,7 @@
     heads = width // HEAD_DIM
     owned = n // heads
     most = 2 * (n * owned - n)
-    entries = most + n
+    entries = most + 1 + n
     keep = entries * 2 * rows * rows * 4 <= KEEP_BYTES
     hbm = pl.BlockSpec(memory_space=pl.ANY)
     message = HEAD_DIM + NOTE_ROWS
@@ -393,22 +435,19 @@
             pltpu.VMEM((rows, width), jnp.bfloat16),
             pltpu.VMEM((heads, rows, LANES), jnp.bfloat16),
             pltpu.VMEM((n, rows, LANES), jnp.bfloat16),
-            pltpu.VMEM((n, 2 * rows, LANES), jnp.bfloat16),
             pltpu.VMEM((n, HEAD_DIM, rows), jnp.bfloat16),
             pltpu.SMEM((n, n), jnp.int32),
-            pltpu.SMEM((n * n + 1,), jnp.int32),
             pltpu.SMEM((n * n + 2,), jnp.int32),
+            pltpu.SMEM((n * n,), jnp.int32),
             pltpu.SMEM((most,), jnp.int32),
             pltpu.SMEM((most,), jnp.int32),
             pltpu.SMEM((most,), jnp.int32),
-            pltpu.SMEM((most,), jnp.int32),
-            pltpu.VMEM((entries, rows), jnp.int32),
             pltpu.VMEM((5, entries, rows), jnp.float32),
+            pltpu.VMEM((2, n, rows), jnp.float32),
+            pltpu.VMEM((2, n, rows), jnp.float32),
             pltpu.VMEM((2, entries, rows), jnp.float32),
             pltpu.VMEM((entries if keep else 1, 2, rows, rows), jnp.float32),
-            pltpu.VMEM((entries, rows, rows), jnp.bfloat16),
-            pltpu.VMEM((most, HEAD_DIM, rows), jnp.float32),
-            pltpu.VMEM((8, LANES), jnp.float32),
+            pltpu.VMEM((entries, HEAD_DIM, rows), jnp.float32),
             pltpu.VMEM((n, message, rows), jnp.bfloat16),
             pltpu.SemaphoreType.DMA((2,)),
             pltpu.SemaphoreType.DMA,

time: 15.7 us -> 15 us (0.955)
  Pallas kernels: 14.9 us -> 14.1 us
    pallas_call x1, Pallas kernels: 14.2 us -> 13.4 us  [per_device(): pl.pallas_call(functools.partial(kernel, n, most, keep), out_shape=pltpu....]
where the time goes in v3:
time: 15 us; the launch traced here: 14.8 us
  Pallas kernels  14.1 us (94%)
  between operations  0.64 us (4%)
    pallas_call x1, Pallas kernels, per_device(): pl.pallas_call(functools.partial(kernel, n, most, keep), out_shape=pltpu....  13.4 us
    pallas_call x1, Pallas kernels, per_device(): pl.pallas_call(unpack, out_shape=(jax.ShapeDtypeStruct((rows, width), jnp...  0.7 us

profile of v3, /device:TPU:0, one launch (start us, length us, event | category | flops | bytes accessed | tf_op | source)
XLA Modules:
  0.0 14.8 jit_solution(10592814858267633173)
XLA Ops:
  0.6 13.4 %distill.1.in_grad = bf16[4,80,128]{2,1,0:T(8,128)(2,1)S(1)} custom-call(bf16[128,256]{1,0:T(8,128)(2,1)} %teacher_hbm.1, bf16[128,256]{1,0:T(8,128)(2,1)} %student_hbm.1, s32[8,8]{1,0:T(8,128)} %table_hbm.1), custom_call_target="tpu_custom_call" | custom-call | tf_op jit(solution)/shard_map/distill/pallas_call | solution.py:428
  14.1 0.7 %unpack.1 = (bf16[128,256]{1,0:T(8,128)(2,1)}, f32[1,4]{1,0:T(1,128)}) custom-call(bf16[4,80,128]{2,1,0:T(8,128)(2,1)S(1)} %distill.1.in_grad), custom_call_target="tpu_custom_call" | custom-call | tf_op jit(solution)/shard_map/unpack/pallas_call | solution.py:464

commit v4 on v3

v4 whole, which is shorter than its diff:
```python
import functools
import math

import jax
import jax.numpy as jnp
from jax import lax
from jax.experimental import pallas as pl
from jax.experimental.pallas import tpu as pltpu
from jax.sharding import PartitionSpec as P

HEAD_DIM = 64
LANES = 128
NOTE_ROWS = 16
KEEP_BYTES = 16 * 1024 * 1024
floor_value = -3e38
distill_weight = 32.0
score_factor = HEAD_DIM ** (-0.5) * math.log2(math.e)
MESH = pl.DeviceIdType.MESH


def repeat(count, body, init=None):
    if count <= 16:
        for step in range(count):
            init = body(step, init)
        return init
    return lax.fori_loop(0, count, body, init)


def kernel(
    n, most, keep, teacher_hbm, student_hbm, table_hbm, grad_out, div_out,
    teacher, student, outbox, own_turned, own_exps, own_stats, inbox, left, turned, arrived,
    table, following, edge_of, edge_row, edge_col, edge_tag,
    stats, peaks, inverses, weights, pieces, exps, shares, out_note, in_note, out_grad, in_grad, near,
    load_sem, table_sem, send_sem, recv_sem, stat_send, stat_recv, note_send, note_recv,
    back_send, back_recv,
):
    rows, width = teacher_hbm.shape
    pairs = width // LANES
    heads = width // HEAD_DIM
    group = LANES // HEAD_DIM
    parts = n // heads
    chips = n // 2
    side = math.isqrt(chips)
    side = side if side * side == chips else 1
    span = chips // side
    me = lax.axis_index("tok")
    head_at = lax.axis_index("head")
    chip, core = me // 2, me % 2
    head = me // parts
    is_worker = me % parts == 0

    def place(step):
        shift, flip = step // 2, step % 2
        high = (chip // span + shift // span) % side
        low = (chip % span + shift % span) % span
        return (high * span + low) * 2 + (core + flip) % 2

    def place_in(worker):
        worker_chip = worker // 2
        high = (chip // span - worker_chip // span + side) % side
        low = (chip % span - worker_chip % span + span) % span
        return (high * span + low) * 2 + (core - worker % 2 + 2) % 2

    def remote(src, dst, send, recv, target):
        return pltpu.make_async_remote_copy(
            src_ref=src, dst_ref=dst, send_sem=send, recv_sem=recv,
            device_id=(head_at, target), device_id_type=MESH,
        )

    barrier = pltpu.get_barrier_semaphore()
    loads = [
        pltpu.make_async_copy(teacher_hbm, teacher, load_sem.at[0]),
        pltpu.make_async_copy(student_hbm, student, load_sem.at[1]),
    ]
    for load in loads:
        load.start()
    table_load = pltpu.make_async_copy(table_hbm, table, table_sem)
    table_load.start()

    def greet(target):
        pl.semaphore_signal(barrier, inc=1, device_id=(head_at, target), device_id_type=MESH)

    @pl.when(is_worker)
    def greet_all():
        def greet_one(step, carry):
            greet(place(n - 1 - step))
            return carry

        repeat(n - 1, greet_one)

    @pl.when(jnp.logical_not(is_worker))
    def greet_workers():
        for step in range(heads):
            greet((head + heads - 1 - step) % heads * parts)

    for load in loads:
        load.wait()
    lane = lax.broadcasted_iota(jnp.int32, (rows, LANES), 1)
    lower = lane < HEAD_DIM
    none = jnp.zeros((), jnp.bfloat16)
    for pair in range(pairs):
        columns = pl.ds(pair * LANES, LANES)
        t_pair = teacher[:, columns].astype(jnp.float32)
        s_pair = student[:, columns].astype(jnp.float32)
        outbox[pair * group] = jnp.where(lower, t_pair, pltpu.roll(s_pair, HEAD_DIM, 1)).astype(
            jnp.bfloat16
        )
        outbox[pair * group + 1] = jnp.where(
            lower, pltpu.roll(t_pair, HEAD_DIM, 1), s_pair
        ).astype(jnp.bfloat16)

    def query_copy(to_head, slot):
        return remote(
            outbox.at[to_head], inbox.at[slot], send_sem.at[to_head], recv_sem.at[slot],
            to_head * parts,
        )

    def stat_copy(to_head, slot):
        return remote(
            own_stats.at[to_head], arrived.at[slot], stat_send.at[to_head], stat_recv.at[slot],
            to_head * parts,
        )

    def grad_copy(slot, target):
        return remote(
            out_grad.at[slot], in_grad.at[head], back_send.at[slot], back_recv.at[head], target
        )

    def note_copy(slot, target):
        return remote(
            out_note.at[slot], in_note.at[head], note_send.at[slot], note_recv.at[head], target
        )

    others = [(head + step) % heads for step in range(heads - 1, 0, -1)]
    pl.semaphore_wait(barrier, jnp.where(is_worker, n - 1, heads))
    for to_head in others:
        query_copy(to_head, place_in(to_head * parts)).start()

    @pl.when(jnp.logical_not(is_worker))
    def send_near():
        query_copy(head, place_in(head * parts)).start()

    def masked(block):
        return jnp.where(lower, block, none), jnp.where(lower, none, block)

    def tile(both, block):
        raw = lax.dot_general(
            both, block, (((1,), (1,)), ((), ())), preferred_element_type=jnp.float32
        )
        return raw[:rows], raw[rows:]

    def measured(t_raw, s_raw):
        t_top = jnp.max(t_raw, axis=0, keepdims=True)
        s_top = jnp.max(s_raw, axis=0, keepdims=True)
        t_exp = jnp.exp2((t_raw - t_top) * score_factor)
        s_exp = jnp.exp2((s_raw - s_top) * score_factor)
        lines = (
            t_top,
            s_top,
            jnp.sum(t_exp, axis=0, keepdims=True),
            jnp.sum(s_exp, axis=0, keepdims=True),
            jnp.sum(t_exp * (t_raw - s_raw), axis=0, keepdims=True),
        )
        return t_exp, s_exp, lines

    for turn in range(heads):
        block = outbox[turn]
        own_turned[turn] = block.T[HEAD_DIM:]
        t_exp, s_exp, lines = measured(*tile(jnp.concatenate(masked(block), axis=0), block))
        own_exps[turn, 0] = t_exp
        own_exps[turn, 1] = s_exp
        for line_at, line in enumerate(lines):
            own_stats[turn, pl.ds(line_at, 1), :] = line
        own_stats[turn, pl.ds(len(lines), 8 - len(lines)), :] = jnp.zeros(
            (8 - len(lines), rows), jnp.float32
        )
    for to_head in others:
        stat_copy(to_head, place_in(to_head * parts)).start()
    table_load.wait()

    @pl.when(jnp.logical_not(is_worker))
    def send_near_stats():
        stat_copy(head, place_in(head * parts)).start()

    @pl.when(is_worker)
    def work():
        inbox[0] = outbox[head]
        arrived[0] = own_stats[head]
        codes = n * n
        blank = most

        def lower_cells(row, body, init):
            if isinstance(row, int):
                for col in range(row):
                    init = body(col, init)
                return init
            return lax.fori_loop(0, row, body, init)

        def count_row(row, count):
            row_at = place(row)

            def count_cell(col, count):
                inside = table[row_at, place(col)] >= 0
                edge = jnp.minimum(2 * count, most - 2)
                edge_of[row * n + col] = jnp.where(inside, edge, blank)
                edge_of[col * n + row] = jnp.where(inside, edge + 1, blank)
                return count + jnp.where(inside, 1, 0)

            return lower_cells(row, count_cell, count)

        repeat(n, count_row, jnp.int32(0))
        following[codes] = jnp.int32(codes)
        following[codes + 1] = jnp.int32(codes)

        def link_row(step, after):
            row = n - 1 - step
            row_at = place(row)
            following[row * n + row] = after

            def link_cell(back, after):
                col = row - 1 - back
                code = row * n + col
                after = jnp.where(table[row_at, place(col)] >= 0, code, after)
                following[code] = after
                return after

            return lower_cells(row, link_cell, after)

        repeat(n, link_row, jnp.int32(codes))

        def list_pair(pair, code):
            code = following[code]
            held = jnp.minimum(code, codes - 1)
            high, low = held // n, held % n
            edge_row[2 * pair] = high
            edge_col[2 * pair] = low
            edge_tag[2 * pair] = jnp.where(code < codes, high, -1)
            edge_row[2 * pair + 1] = low
            edge_col[2 * pair + 1] = high
            edge_tag[2 * pair + 1] = jnp.where(code < codes, low, -1)
            return code + 1

        repeat(most // 2, list_pair, jnp.int32(0))
        shares[blank] = jnp.zeros((HEAD_DIM, rows), jnp.float32)

        def take_block(slot, carry):
            @pl.when(slot > 0)
            def wait_block():
                remote(
                    outbox.at[0], inbox.at[slot], send_sem.at[0], recv_sem.at[slot], place(slot)
                ).wait_recv()

            return carry

        def keep_block(slot, carry):
            block = inbox[slot]
            t_part, s_part = masked(block)
            left[slot, pl.ds(0, rows), :] = t_part
            left[slot, pl.ds(rows, rows), :] = s_part
            turned[slot] = block.T[HEAD_DIM:]
            return carry

        def take_chip(shift, carry):
            for inner in range(2):
                take_block(2 * shift + inner, None)
            for inner in range(2):
                keep_block(2 * shift + inner, None)
            return carry

        repeat(chips, take_chip)

        def measure_edge(edge, carry):
            t_exp, s_exp, lines = measured(*tile(left[edge_col[edge]], inbox[edge_row[edge]]))
            for line_at, line in enumerate(lines):
                stats[line_at, pl.ds(edge, 1), :] = line
            if keep:
                exps[edge, 0] = t_exp
                exps[edge, 1] = s_exp
            return carry

        repeat(most, measure_edge)

        def take_stats(step, carry):
            slot = step + 1
            remote(
                own_stats.at[0], arrived.at[slot], stat_send.at[0], stat_recv.at[slot], place(slot)
            ).wait_recv()
            return carry

        repeat(n - 1, take_stats)
        slot_row = lax.broadcasted_iota(jnp.int32, (n, rows), 0)

        def place_stats(slot, carry):
            return tuple(
                jnp.where(slot_row == slot, arrived[slot, pl.ds(line_at, 1), :], line)
                for line_at, line in enumerate(carry)
            )

        blank_lines = jnp.zeros((n, rows), jnp.float32)
        first_stats = repeat(n, place_stats, (blank_lines,) * 5)

        def raise_peaks(edge, carry):
            mine = slot_row == edge_tag[edge]
            at = pl.ds(edge, 1)
            return tuple(
                jnp.maximum(peak, jnp.where(mine, stats[which, at, :], floor_value))
                for which, peak in enumerate(carry)
            )

        tops = repeat(most, raise_peaks, first_stats[:2])
        for which in range(2):
            peaks[which] = tops[which]
        first_parts = [
            jnp.exp2((first_stats[which] - tops[which]) * score_factor) for which in range(2)
        ]
        sums = (
            first_parts[0] * first_stats[2],
            first_parts[0] * first_stats[4],
            first_parts[1] * first_stats[3],
        )

        def add_edge(edge, carry):
            tag = edge_tag[edge]
            mine = slot_row == tag
            at = pl.ds(edge, 1)
            fresh = []
            for which in range(2):
                peak = peaks[which, pl.ds(jnp.maximum(tag, 0), 1), :]
                part = jnp.exp2(jnp.minimum((stats[which, at, :] - peak) * score_factor, 0.0))
                weights[which, at, :] = part
                fresh.append(part * stats[2 + which, at, :])
                if which == 0:
                    fresh.append(part * stats[4, at, :])
            return tuple(
                total + jnp.where(mine, piece, 0.0)
                for total, piece in zip(carry, fresh, strict=True)
            )

        t_sum, cross, s_sum = repeat(most, add_edge, sums)
        t_inverse, s_inverse = 1.0 / t_sum, 1.0 / s_sum
        inverses[0] = t_inverse
        inverses[1] = s_inverse

        def weigh_edge(edge, carry):
            tag = edge_tag[edge]
            at, mine_at = pl.ds(edge, 1), pl.ds(jnp.maximum(tag, 0), 1)
            valid = jnp.where(tag >= 0, 1.0, 0.0)
            for which in range(2):
                weights[which, at, :] = weights[which, at, :] * (
                    inverses[which, mine_at, :] * valid
                )
            return carry

        repeat(most, weigh_edge)

        def split(value):
            first = value.astype(jnp.bfloat16).astype(jnp.float32)
            second = (value - first).astype(jnp.bfloat16).astype(jnp.float32)
            return [first, second, value - first - second]

        for which in range(2):
            for at, piece in enumerate(split(first_parts[which] * inverses[which])):
                pieces[3 * which + at] = piece
        total = (
            (cross * t_inverse - tops[0] + tops[1]) * score_factor
            - jnp.log2(t_sum)
            + jnp.log2(s_sum)
        )
        total = jnp.sum(jnp.sum(total, axis=0, keepdims=True), axis=1, keepdims=True) * (
            math.log(2.0) / (rows * n)
        )
        note_row = lax.broadcasted_iota(jnp.int32, (NOTE_ROWS, LANES), 0)
        base = jnp.zeros((NOTE_ROWS, LANES), jnp.float32)
        for at, piece in enumerate(split(total)):
            base = jnp.where(note_row == at, piece, base)

        def send_note(step, carry):
            slot = n - 1 - step
            note = base
            for at in range(6):
                note = jnp.where(note_row == 3 + at, pieces[at, pl.ds(slot, 1), :], note)
            out_note[slot] = note.astype(jnp.bfloat16)

            @pl.when(slot > 0)
            def start_note():
                note_copy(slot, place(slot)).start()

            return carry

        repeat(n, send_note)

        def gap_of(edge, col, row):
            at = pl.ds(edge, 1)
            if keep:
                t_exp, s_exp = exps[edge, 0], exps[edge, 1]
            else:
                t_raw, s_raw = tile(left[col], inbox[row])
                t_exp = jnp.exp2((t_raw - stats[0, at, :]) * score_factor)
                s_exp = jnp.exp2((s_raw - stats[1, at, :]) * score_factor)
            return s_exp * weights[1, at, :] - t_exp * weights[0, at, :]

        def share_pair(pair, carry):
            high, low = edge_row[2 * pair], edge_col[2 * pair]
            gap = gap_of(2 * pair, low, high)
            back = gap_of(2 * pair + 1, high, low)
            symmetric = (gap + back.T).astype(jnp.bfloat16)
            shares[2 * pair] = jnp.dot(turned[low], symmetric, preferred_element_type=jnp.float32)
            shares[2 * pair + 1] = lax.dot_general(
                turned[high], symmetric, (((1,), (1,)), ((), ())),
                preferred_element_type=jnp.float32,
            )
            return carry

        repeat(most // 2, share_pair)

        def finish(step, carry):
            slot = n - 1 - step

            def add_share(turn, line):
                fresh = shares[edge_of[slot * n + (slot + turn + 1) % n]]
                return fresh if line is None else line + fresh

            line = repeat(n - 1, add_share, None if n <= 16 else jnp.zeros((HEAD_DIM, rows), jnp.float32))
            out_grad[slot] = (line * (distill_weight * HEAD_DIM ** (-0.5))).astype(jnp.bfloat16)

            @pl.when(slot > 0)
            def send_grad():
                grad_copy(slot, place(slot)).start()

            return carry

        repeat(n, finish)
        in_note[head] = out_note[0]
        in_grad[head] = out_grad[0]

    def take(kind, sends, receives, buffers, step):
        from_head = (head + step) % heads

        def take_one():
            remote(
                kind.at[0], buffers.at[from_head], sends.at[0], receives.at[from_head],
                from_head * parts,
            ).wait_recv()

        if step == 0:
            pl.when(jnp.logical_not(is_worker))(take_one)
        else:
            take_one()
        return from_head

    for step in range(heads):
        take(out_note, note_send, note_recv, in_note, step)
    for turn in range(heads):
        note = in_note[turn].astype(jnp.float32)
        t_weight = note[3:4] + note[4:5] + note[5:6]
        s_weight = note[6:7] + note[7:8] + note[8:9]
        gap = own_exps[turn, 1] * s_weight - own_exps[turn, 0] * t_weight
        symmetric = (gap + gap.T).astype(jnp.bfloat16)
        near[turn] = jnp.dot(own_turned[turn], symmetric, preferred_element_type=jnp.float32) * (
            distill_weight * HEAD_DIM ** (-0.5)
        )
        div_out[pl.ds(turn, 1), :] = note[0:1] + note[1:2] + note[2:3]
    for step in range(heads):
        from_head = take(out_grad, back_send, back_recv, in_grad, step)
        grad_out[from_head] = (in_grad[from_head].astype(jnp.float32) + near[from_head]).astype(
            jnp.bfloat16
        )

    for to_head in others:
        query_copy(to_head, 0).wait_send()
        stat_copy(to_head, 0).wait_send()

    @pl.when(jnp.logical_not(is_worker))
    def drain_near():
        query_copy(head, 0).wait_send()
        stat_copy(head, 0).wait_send()

    @pl.when(is_worker)
    def drain_back():
        def drain_grads(step, carry):
            note_copy(step + 1, place(step + 1)).wait_send()
            grad_copy(step + 1, place(step + 1)).wait_send()
            return carry

        repeat(n - 1, drain_grads)


def unpack(in_grad, in_div, grad_ref, div_ref):
    heads = in_grad.shape[0]
    group = LANES // HEAD_DIM
    for pair in range(heads // group):
        both = jnp.concatenate([in_grad[pair * group + inner] for inner in range(group)], axis=0)
        grad_ref[:, pl.ds(pair * LANES, LANES)] = both.T
    div_lane = lax.broadcasted_iota(jnp.int32, (1, LANES), 1)
    div_row = jnp.zeros((1, LANES), jnp.float32)
    for slot in range(heads):
        div_row = jnp.where(div_lane == slot, in_div[pl.ds(slot, 1), :], div_row)
    div_ref[...] = div_row[:, :heads]


def per_device(n, teacher_q, student_q, owner_table):
    rows, width = teacher_q.shape
    heads = width // HEAD_DIM
    owned = n // heads
    most = 2 * (n * owned - n)
    keep = most * 2 * rows * rows * 4 <= KEEP_BYTES
    hbm = pl.BlockSpec(memory_space=pl.ANY)
    vmem = pl.BlockSpec(memory_space=pltpu.VMEM)
    packed = pl.pallas_call(
        functools.partial(kernel, n, most, keep),
        out_shape=(
            pltpu.VMEM((heads, HEAD_DIM, rows), jnp.bfloat16),
            pltpu.VMEM((heads, rows), jnp.float32),
        ),
        in_specs=[hbm, hbm, hbm],
        out_specs=(vmem, vmem),
        scratch_shapes=[
            pltpu.VMEM((rows, width), jnp.bfloat16),
            pltpu.VMEM((rows, width), jnp.bfloat16),
            pltpu.VMEM((heads, rows, LANES), jnp.bfloat16),
            pltpu.VMEM((heads, HEAD_DIM, rows), jnp.bfloat16),
            pltpu.VMEM((heads, 2, rows, rows), jnp.float32),
            pltpu.VMEM((heads, 8, rows), jnp.float32),
            pltpu.VMEM((n, rows, LANES), jnp.bfloat16),
            pltpu.VMEM((n, 2 * rows, LANES), jnp.bfloat16),
            pltpu.VMEM((n, HEAD_DIM, rows), jnp.bfloat16),
            pltpu.VMEM((n, 8, rows), jnp.float32),
            pltpu.SMEM((n, n), jnp.int32),
            pltpu.SMEM((n * n + 2,), jnp.int32),
            pltpu.SMEM((n * n,), jnp.int32),
            pltpu.SMEM((most,), jnp.int32),
            pltpu.SMEM((most,), jnp.int32),
            pltpu.SMEM((most,), jnp.int32),
            pltpu.VMEM((5, most, rows), jnp.float32),
            pltpu.VMEM((2, n, rows), jnp.float32),
            pltpu.VMEM((2, n, rows), jnp.float32),
            pltpu.VMEM((2, most, rows), jnp.float32),
            pltpu.VMEM((6, n, rows), jnp.float32),
            pltpu.VMEM((most if keep else 1, 2, rows, rows), jnp.float32),
            pltpu.VMEM((most + 1, HEAD_DIM, rows), jnp.float32),
            pltpu.VMEM((n, NOTE_ROWS, rows), jnp.bfloat16),
            pltpu.VMEM((heads, NOTE_ROWS, rows), jnp.bfloat16),
            pltpu.VMEM((n, HEAD_DIM, rows), jnp.bfloat16),
            pltpu.VMEM((heads, HEAD_DIM, rows), jnp.bfloat16),
            pltpu.VMEM((heads, HEAD_DIM, rows), jnp.float32),
            pltpu.SemaphoreType.DMA((2,)),
            pltpu.SemaphoreType.DMA,
            pltpu.SemaphoreType.DMA((heads,)),
            pltpu.SemaphoreType.DMA((n,)),
            pltpu.SemaphoreType.DMA((heads,)),
            pltpu.SemaphoreType.DMA((n,)),
            pltpu.SemaphoreType.DMA((n,)),
            pltpu.SemaphoreType.DMA((heads,)),
            pltpu.SemaphoreType.DMA((n,)),
            pltpu.SemaphoreType.DMA((heads,)),
        ],
        compiler_params=pltpu.CompilerParams(
            collective_id=0, has_side_effects=True, vmem_limit_bytes=60 * 1024 * 1024
        ),
        name="distill",
    )(*[pltpu.with_memory_space_constraint(x, pltpu.HBM) for x in (teacher_q, student_q, owner_table)])
    grad, divergence = pl.pallas_call(
        unpack,
        out_shape=(
            jax.ShapeDtypeStruct((rows, width), jnp.bfloat16),
            jax.ShapeDtypeStruct((1, heads), jnp.float32),
        ),
        in_specs=[vmem, vmem],
        out_specs=(vmem, vmem),
        compiler_params=pltpu.CompilerParams(vmem_limit_bytes=4 * 1024 * 1024),
        name="unpack",
    )(*packed)
    return (grad, divergence.reshape(heads))


def solution(mesh):
    placed = (P("tok", "head"), P("tok", "head"), P())
    return jax.shard_map(
        functools.partial(per_device, mesh.shape["tok"]),
        mesh=mesh,
        in_specs=placed,
        out_specs=(P("tok", "head"), P("head")),
        check_vma=False,
    )
```

time: 15 us -> 14.3 us (0.953)
  Pallas kernels: 14.1 us -> 13.5 us
    pallas_call x1, Pallas kernels: 13.4 us -> 12.8 us  [per_device(): pl.pallas_call(functools.partial(kernel, n, most, keep), out_shape=(pltpu...]
where the time goes in v4:
time: 14.3 us; the launch traced here: 14.2 us
  Pallas kernels  13.5 us (94%)
  between operations  0.64 us (4%)
    pallas_call x1, Pallas kernels, per_device(): pl.pallas_call(functools.partial(kernel, n, most, keep), out_shape=(pltpu...  12.8 us
    pallas_call x1, Pallas kernels, per_device(): pl.pallas_call(unpack, out_shape=(jax.ShapeDtypeStruct((rows, width), jnp...  0.7 us

profile of v4, /device:TPU:0, one launch (start us, length us, event | category | flops | bytes accessed | tf_op | source)
XLA Modules:
  0.0 14.2 jit_solution(15269312837488079327)
XLA Ops:
  0.6 12.8 %distill.1 = (bf16[4,64,128]{2,1,0:T(8,128)(2,1)S(1)}, f32[4,128]{1,0:T(4,128)S(1)}) custom-call(bf16[128,256]{1,0:T(8,128)(2,1)} %teacher_hbm.1, bf16[128,256]{1,0:T(8,128)(2,1)} %student_hbm.1, s32[8,8]{1,0:T(8,128)} %table_hbm.1), custom_call_target="tpu_custom_call" | custom-call | tf_op jit(solution)/shard_map/distill/pallas_call | solution.py:509
  13.5 0.7 %unpack.1 = (bf16[128,256]{1,0:T(8,128)(2,1)}, f32[1,4]{1,0:T(1,128)}) custom-call(bf16[4,64,128]{2,1,0:T(8,128)(2,1)S(1)} %get-tuple-element.6.in_grad, f32[4,128]{1,0:T(4,128)S(1)} %get-tuple-element.7.in_div), custom_call_target="tpu_custom_call" | custom-call | tf_op jit(solution)/shard_map/unpack/pallas_call | solution.py:562

commit v5 on v4

--- a/solution.py
+++ b/solution.py
@@ -40,26 +40,26 @@
     group = LANES // HEAD_DIM
     parts = n // heads
     chips = n // 2
-    side = math.isqrt(chips)
-    side = side if side * side == chips else 1
-    span = chips // side
+
+    def worker_of(of_head):
+        return of_head * parts + 1
+
     me = lax.axis_index("tok")
     head_at = lax.axis_index("head")
-    chip, core = me // 2, me % 2
-    head = me // parts
-    is_worker = me % parts == 0
+    chip, core = lax.div(me, 2), lax.rem(me, 2)
+    head = lax.div(me, parts)
+    is_worker = me == worker_of(head)
+    way = 1 - 2 * lax.rem(chip, 2)
 
     def place(step):
-        shift, flip = step // 2, step % 2
-        high = (chip // span + shift // span) % side
-        low = (chip % span + shift % span) % span
-        return (high * span + low) * 2 + (core + flip) % 2
+        shift, flip = (step // 2, step % 2) if isinstance(step, int) else (lax.div(step, 2), lax.rem(step, 2))
+        return 2 * lax.rem(chip + way * shift + chips, chips) + lax.rem(core + flip, 2)
 
     def place_in(worker):
-        worker_chip = worker // 2
-        high = (chip // span - worker_chip // span + side) % side
-        low = (chip % span - worker_chip % span + span) % span
-        return (high * span + low) * 2 + (core - worker % 2 + 2) % 2
+        worker_chip = lax.div(worker, 2)
+        worker_way = 1 - 2 * lax.rem(worker_chip, 2)
+        shift = lax.rem(worker_way * (chip - worker_chip) + chips, chips)
+        return 2 * shift + lax.rem(core + lax.rem(worker, 2), 2)
 
     def remote(src, dst, send, recv, target):
         return pltpu.make_async_remote_copy(
@@ -91,7 +91,7 @@
     @pl.when(jnp.logical_not(is_worker))
     def greet_workers():
         for step in range(heads):
-            greet((head + heads - 1 - step) % heads * parts)
+            greet(worker_of(lax.rem(head + heads - 1 - step, heads)))
 
     for load in loads:
         load.wait()
@@ -112,13 +112,13 @@
     def query_copy(to_head, slot):
         return remote(
             outbox.at[to_head], inbox.at[slot], send_sem.at[to_head], recv_sem.at[slot],
-            to_head * parts,
+            worker_of(to_head),
         )
 
     def stat_copy(to_head, slot):
         return remote(
             own_stats.at[to_head], arrived.at[slot], stat_send.at[to_head], stat_recv.at[slot],
-            to_head * parts,
+            worker_of(to_head),
         )
 
     def grad_copy(slot, target):
@@ -131,14 +131,14 @@
             out_note.at[slot], in_note.at[head], note_send.at[slot], note_recv.at[head], target
         )
 
-    others = [(head + step) % heads for step in range(heads - 1, 0, -1)]
+    others = [lax.rem(head + step, heads) for step in range(heads - 1, 0, -1)]
     pl.semaphore_wait(barrier, jnp.where(is_worker, n - 1, heads))
     for to_head in others:
-        query_copy(to_head, place_in(to_head * parts)).start()
+        query_copy(to_head, place_in(worker_of(to_head))).start()
 
     @pl.when(jnp.logical_not(is_worker))
     def send_near():
-        query_copy(head, place_in(head * parts)).start()
+        query_copy(head, place_in(worker_of(head))).start()
 
     def masked(block):
         return jnp.where(lower, block, none), jnp.where(lower, none, block)
@@ -175,12 +175,12 @@
             (8 - len(lines), rows), jnp.float32
         )
     for to_head in others:
-        stat_copy(to_head, place_in(to_head * parts)).start()
+        stat_copy(to_head, place_in(worker_of(to_head))).start()
     table_load.wait()
 
     @pl.when(jnp.logical_not(is_worker))
     def send_near_stats():
-        stat_copy(head, place_in(head * parts)).start()
+        stat_copy(head, place_in(worker_of(head))).start()
 
     @pl.when(is_worker)
     def work():
@@ -231,7 +231,7 @@
         def list_pair(pair, code):
             code = following[code]
             held = jnp.minimum(code, codes - 1)
-            high, low = held // n, held % n
+            high, low = lax.div(held, n), lax.rem(held, n)
             edge_row[2 * pair] = high
             edge_col[2 * pair] = low
             edge_tag[2 * pair] = jnp.where(code < codes, high, -1)
@@ -434,12 +434,12 @@
         in_grad[head] = out_grad[0]
 
     def take(kind, sends, receives, buffers, step):
-        from_head = (head + step) % heads
+        from_head = lax.rem(head + step, heads)
 
         def take_one():
             remote(
                 kind.at[0], buffers.at[from_head], sends.at[0], receives.at[from_head],
-                from_head * parts,
+                worker_of(from_head),
             ).wait_recv()
 
         if step == 0:

time: 14.3 us -> 13.2 us (0.923)
  Pallas kernels: 13.5 us -> 12.4 us
    pallas_call x1, Pallas kernels: 12.8 us -> 11.6 us  [per_device(): pl.pallas_call(functools.partial(kernel, n, most, keep), out_shape=(pltpu...]
where the time goes in v5:
time: 13.2 us; the launch traced here: 13 us
  Pallas kernels  12.4 us (94%)
  between operations  0.64 us (5%)
    pallas_call x1, Pallas kernels, per_device(): pl.pallas_call(functools.partial(kernel, n, most, keep), out_shape=(pltpu...  11.6 us
    pallas_call x1, Pallas kernels, per_device(): pl.pallas_call(unpack, out_shape=(jax.ShapeDtypeStruct((rows, width), jnp...  0.7 us

profile of v5, /device:TPU:0, one launch (start us, length us, event | category | flops | bytes accessed | tf_op | source)
XLA Modules:
  0.0 13.0 jit_solution(2101422946295392449)
XLA Ops:
  0.6 11.6 %distill.1 = (bf16[4,64,128]{2,1,0:T(8,128)(2,1)S(1)}, f32[4,128]{1,0:T(4,128)S(1)}) custom-call(bf16[128,256]{1,0:T(8,128)(2,1)} %teacher_hbm.1, bf16[128,256]{1,0:T(8,128)(2,1)} %student_hbm.1, s32[8,8]{1,0:T(8,128)} %table_hbm.1), custom_call_target="tpu_custom_call" | custom-call | tf_op jit(solution)/shard_map/distill/pallas_call | solution.py:509
  12.3 0.7 %unpack.1 = (bf16[128,256]{1,0:T(8,128)(2,1)}, f32[1,4]{1,0:T(1,128)}) custom-call(bf16[4,64,128]{2,1,0:T(8,128)(2,1)S(1)} %get-tuple-element.6.in_grad, f32[4,128]{1,0:T(4,128)S(1)} %get-tuple-element.7.in_div), custom_call_target="tpu_custom_call" | custom-call | tf_op jit(solution)/shard_map/unpack/pallas_call | solution.py:562

commit v6 on v5

--- a/solution.py
+++ b/solution.py
@@ -111,25 +111,29 @@
 
     def query_copy(to_head, slot):
         return remote(
-            outbox.at[to_head], inbox.at[slot], send_sem.at[to_head], recv_sem.at[slot],
+            outbox.at[to_head], inbox.at[slot], send_sem, recv_sem.at[lax.div(slot, 2)],
             worker_of(to_head),
         )
 
     def stat_copy(to_head, slot):
         return remote(
-            own_stats.at[to_head], arrived.at[slot], stat_send.at[to_head], stat_recv.at[slot],
+            own_stats.at[to_head], arrived.at[slot], stat_send, stat_recv,
             worker_of(to_head),
         )
 
     def grad_copy(slot, target):
         return remote(
-            out_grad.at[slot], in_grad.at[head], back_send.at[slot], back_recv.at[head], target
+            out_grad.at[slot], in_grad.at[head], back_send, back_recv, target
         )
 
     def note_copy(slot, target):
         return remote(
-            out_note.at[slot], in_note.at[head], note_send.at[slot], note_recv.at[head], target
-        )
+            out_note.at[slot], in_note.at[head], note_send, note_recv, target
+        )
+
+    def all_of(ref, first, count, sem):
+        whole = ref.at[pl.ds(first, count)]
+        return remote(whole, whole, sem, sem, me)
 
     others = [lax.rem(head + step, heads) for step in range(heads - 1, 0, -1)]
     pl.semaphore_wait(barrier, jnp.where(is_worker, n - 1, heads))
@@ -243,15 +247,6 @@
         repeat(most // 2, list_pair, jnp.int32(0))
         shares[blank] = jnp.zeros((HEAD_DIM, rows), jnp.float32)
 
-        def take_block(slot, carry):
-            @pl.when(slot > 0)
-            def wait_block():
-                remote(
-                    outbox.at[0], inbox.at[slot], send_sem.at[0], recv_sem.at[slot], place(slot)
-                ).wait_recv()
-
-            return carry
-
         def keep_block(slot, carry):
             block = inbox[slot]
             t_part, s_part = masked(block)
@@ -261,13 +256,20 @@
             return carry
 
         def take_chip(shift, carry):
-            for inner in range(2):
-                take_block(2 * shift + inner, None)
+            if isinstance(shift, int) and shift == 0:
+                all_of(inbox, 1, 1, recv_sem.at[0]).wait_recv()
+            else:
+                all_of(inbox, 2 * shift, 2, recv_sem.at[shift]).wait_recv()
             for inner in range(2):
                 keep_block(2 * shift + inner, None)
             return carry
 
-        repeat(chips, take_chip)
+        take_chip(0, None)
+        if chips > 16:
+            lax.fori_loop(1, chips, take_chip, None)
+        else:
+            for shift in range(1, chips):
+                take_chip(shift, None)
 
         def measure_edge(edge, carry):
             t_exp, s_exp, lines = measured(*tile(left[edge_col[edge]], inbox[edge_row[edge]]))
@@ -280,14 +282,7 @@
 
         repeat(most, measure_edge)
 
-        def take_stats(step, carry):
-            slot = step + 1
-            remote(
-                own_stats.at[0], arrived.at[slot], stat_send.at[0], stat_recv.at[slot], place(slot)
-            ).wait_recv()
-            return carry
-
-        repeat(n - 1, take_stats)
+        all_of(arrived, 1, n - 1, stat_recv).wait_recv()
         slot_row = lax.broadcasted_iota(jnp.int32, (n, rows), 0)
 
         def place_stats(slot, carry):
@@ -433,23 +428,16 @@
         in_note[head] = out_note[0]
         in_grad[head] = out_grad[0]
 
-    def take(kind, sends, receives, buffers, step):
-        from_head = lax.rem(head + step, heads)
-
-        def take_one():
-            remote(
-                kind.at[0], buffers.at[from_head], sends.at[0], receives.at[from_head],
-                worker_of(from_head),
-            ).wait_recv()
-
-        if step == 0:
-            pl.when(jnp.logical_not(is_worker))(take_one)
-        else:
-            take_one()
-        return from_head
-
-    for step in range(heads):
-        take(out_note, note_send, note_recv, in_note, step)
+    def take(buffers, sem):
+        @pl.when(is_worker)
+        def take_others():
+            all_of(buffers, 0, heads - 1, sem).wait_recv()
+
+        @pl.when(jnp.logical_not(is_worker))
+        def take_all():
+            all_of(buffers, 0, heads, sem).wait_recv()
+
+    take(in_note, note_recv)
     for turn in range(heads):
         note = in_note[turn].astype(jnp.float32)
         t_weight = note[3:4] + note[4:5] + note[5:6]
@@ -460,29 +448,21 @@
             distill_weight * HEAD_DIM ** (-0.5)
         )
         div_out[pl.ds(turn, 1), :] = note[0:1] + note[1:2] + note[2:3]
-    for step in range(heads):
-        from_head = take(out_grad, back_send, back_recv, in_grad, step)
-        grad_out[from_head] = (in_grad[from_head].astype(jnp.float32) + near[from_head]).astype(
-            jnp.bfloat16
-        )
-
-    for to_head in others:
-        query_copy(to_head, 0).wait_send()
-        stat_copy(to_head, 0).wait_send()
+    take(in_grad, back_recv)
+    for turn in range(heads):
+        grad_out[turn] = (in_grad[turn].astype(jnp.float32) + near[turn]).astype(jnp.bfloat16)
+
+    @pl.when(is_worker)
+    def drain_worker():
+        all_of(outbox, 0, heads - 1, send_sem).wait_send()
+        all_of(own_stats, 0, heads - 1, stat_send).wait_send()
+        all_of(out_note, 1, n - 1, note_send).wait_send()
+        all_of(out_grad, 1, n - 1, back_send).wait_send()
 
     @pl.when(jnp.logical_not(is_worker))
-    def drain_near():
-        query_copy(head, 0).wait_send()
-        stat_copy(head, 0).wait_send()
-
-    @pl.when(is_worker)
-    def drain_back():
-        def drain_grads(step, carry):
-            note_copy(step + 1, place(step + 1)).wait_send()
-            grad_copy(step + 1, place(step + 1)).wait_send()
-            return carry
-
-        repeat(n - 1, drain_grads)
+    def drain_server():
+        all_of(outbox, 0, heads, send_sem).wait_send()
+        all_of(own_stats, 0, heads, stat_send).wait_send()
 
 
 def unpack(in_grad, in_div, grad_ref, div_ref):
@@ -501,6 +481,7 @@
 def per_device(n, teacher_q, student_q, owner_table):
     rows, width = teacher_q.shape
     heads = width // HEAD_DIM
+    chips = n // 2
     owned = n // heads
     most = 2 * (n * owned - n)
     keep = most * 2 * rows * rows * 4 <= KEEP_BYTES
@@ -545,14 +526,14 @@
             pltpu.VMEM((heads, HEAD_DIM, rows), jnp.float32),
             pltpu.SemaphoreType.DMA((2,)),
             pltpu.SemaphoreType.DMA,
-            pltpu.SemaphoreType.DMA((heads,)),
-            pltpu.SemaphoreType.DMA((n,)),
-            pltpu.SemaphoreType.DMA((heads,)),
-            pltpu.SemaphoreType.DMA((n,)),
-            pltpu.SemaphoreType.DMA((n,)),
-            pltpu.SemaphoreType.DMA((heads,)),
-            pltpu.SemaphoreType.DMA((n,)),
-            pltpu.SemaphoreType.DMA((heads,)),
+            pltpu.SemaphoreType.DMA,
+            pltpu.SemaphoreType.DMA((chips,)),
+            pltpu.SemaphoreType.DMA,
+            pltpu.SemaphoreType.DMA,
+            pltpu.SemaphoreType.DMA,
+            pltpu.SemaphoreType.DMA,
+            pltpu.SemaphoreType.DMA,
+            pltpu.SemaphoreType.DMA,
         ],
         compiler_params=pltpu.CompilerParams(
             collective_id=0, has_side_effects=True, vmem_limit_bytes=60 * 1024 * 1024

time: 13.2 us -> 12.8 us (0.970)
  Pallas kernels: 12.4 us -> 12 us
    pallas_call x1, Pallas kernels: 11.6 us -> 11.3 us  [per_device(): pl.pallas_call(functools.partial(kernel, n, most, keep), out_shape=(pltpu...]
where the time goes in v6:
time: 12.8 us; the launch traced here: 12.6 us
  Pallas kernels  12 us (94%)
  between operations  0.64 us (5%)
    pallas_call x1, Pallas kernels, per_device(): pl.pallas_call(functools.partial(kernel, n, most, keep), out_shape=(pltpu...  11.3 us
    pallas_call x1, Pallas kernels, per_device(): pl.pallas_call(unpack, out_shape=(jax.ShapeDtypeStruct((rows, width), jnp...  0.7 us

profile of v6, /device:TPU:0, one launch (start us, length us, event | category | flops | bytes accessed | tf_op | source)
XLA Modules:
  0.0 12.6 jit_solution(16942859685770511097)
XLA Ops:
  0.6 11.3 %distill.1 = (bf16[4,64,128]{2,1,0:T(8,128)(2,1)S(1)}, f32[4,128]{1,0:T(4,128)S(1)}) custom-call(bf16[128,256]{1,0:T(8,128)(2,1)} %teacher_hbm.1, bf16[128,256]{1,0:T(8,128)(2,1)} %student_hbm.1, s32[8,8]{1,0:T(8,128)} %table_hbm.1), custom_call_target="tpu_custom_call" | custom-call | tf_op jit(solution)/shard_map/distill/pallas_call | solution.py:490
  11.9 0.7 %unpack.1 = (bf16[128,256]{1,0:T(8,128)(2,1)}, f32[1,4]{1,0:T(1,128)}) custom-call(bf16[4,64,128]{2,1,0:T(8,128)(2,1)S(1)} %get-tuple-element.6.in_grad, f32[4,128]{1,0:T(4,128)S(1)} %get-tuple-element.7.in_div), custom_call_target="tpu_custom_call" | custom-call | tf_op jit(solution)/shard_map/unpack/pallas_call | solution.py:543

commit v7 on v6

--- a/solution.py
+++ b/solution.py
@@ -42,7 +42,7 @@
     chips = n // 2
 
     def worker_of(of_head):
-        return of_head * parts + 1
+        return jnp.where(of_head == 0, 0, of_head * parts + 1)
 
     me = lax.axis_index("tok")
     head_at = lax.axis_index("head")
@@ -135,7 +135,7 @@
         whole = ref.at[pl.ds(first, count)]
         return remote(whole, whole, sem, sem, me)
 
-    others = [lax.rem(head + step, heads) for step in range(heads - 1, 0, -1)]
+    others = [lax.rem(head + way * step + heads, heads) for step in (3, 1, 2)]
     pl.semaphore_wait(barrier, jnp.where(is_worker, n - 1, heads))
     for to_head in others:
         query_copy(to_head, place_in(worker_of(to_head))).start()
@@ -448,10 +448,6 @@
             distill_weight * HEAD_DIM ** (-0.5)
         )
         div_out[pl.ds(turn, 1), :] = note[0:1] + note[1:2] + note[2:3]
-    take(in_grad, back_recv)
-    for turn in range(heads):
-        grad_out[turn] = (in_grad[turn].astype(jnp.float32) + near[turn]).astype(jnp.bfloat16)
-
     @pl.when(is_worker)
     def drain_worker():
         all_of(outbox, 0, heads - 1, send_sem).wait_send()
@@ -463,6 +459,10 @@
     def drain_server():
         all_of(outbox, 0, heads, send_sem).wait_send()
         all_of(own_stats, 0, heads, stat_send).wait_send()
+
+    take(in_grad, back_recv)
+    for turn in range(heads):
+        grad_out[turn] = (in_grad[turn].astype(jnp.float32) + near[turn]).astype(jnp.bfloat16)
 
 
 def unpack(in_grad, in_div, grad_ref, div_ref):

time: 12.8 us -> 12.7 us (level)
  no operation moved by 1% of the time
where the time goes in v7:
time: 12.7 us; the launch traced here: 12.5 us
  Pallas kernels  11.9 us (94%)
  between operations  0.64 us (5%)
    pallas_call x1, Pallas kernels, per_device(): pl.pallas_call(functools.partial(kernel, n, most, keep), out_shape=(pltpu...  11.2 us
    pallas_call x1, Pallas kernels, per_device(): pl.pallas_call(unpack, out_shape=(jax.ShapeDtypeStruct((rows, width), jnp...  0.7 us

profile of v7, /device:TPU:0, one launch (start us, length us, event | category | flops | bytes accessed | tf_op | source)
XLA Modules:
  0.0 12.5 jit_solution(13901724089167046018)
XLA Ops:
  0.6 11.2 %distill.1 = (bf16[4,64,128]{2,1,0:T(8,128)(2,1)S(1)}, f32[4,128]{1,0:T(4,128)S(1)}) custom-call(bf16[128,256]{1,0:T(8,128)(2,1)} %teacher_hbm.1, bf16[128,256]{1,0:T(8,128)(2,1)} %student_hbm.1, s32[8,8]{1,0:T(8,128)} %table_hbm.1), custom_call_target="tpu_custom_call" | custom-call | tf_op jit(solution)/shard_map/distill/pallas_call | solution.py:490
  11.8 0.7 %unpack.1 = (bf16[128,256]{1,0:T(8,128)(2,1)}, f32[1,4]{1,0:T(1,128)}) custom-call(bf16[4,64,128]{2,1,0:T(8,128)(2,1)S(1)} %get-tuple-element.6.in_grad, f32[4,128]{1,0:T(4,128)S(1)} %get-tuple-element.7.in_div), custom_call_target="tpu_custom_call" | custom-call | tf_op jit(solution)/shard_map/unpack/pallas_call | solution.py:543

commit v8 on v7

--- a/solution.py
+++ b/solution.py
@@ -28,7 +28,7 @@
 
 def kernel(
     n, most, keep, teacher_hbm, student_hbm, table_hbm, grad_out, div_out,
-    teacher, student, outbox, own_turned, own_exps, own_stats, inbox, left, turned, arrived,
+    queries, outbox, own_turned, own_exps, own_stats, inbox, left, turned, arrived,
     table, following, edge_of, edge_row, edge_col, edge_tag,
     stats, peaks, inverses, weights, pieces, exps, shares, out_note, in_note, out_grad, in_grad, near,
     load_sem, table_sem, send_sem, recv_sem, stat_send, stat_recv, note_send, note_recv,
@@ -69,8 +69,8 @@
 
     barrier = pltpu.get_barrier_semaphore()
     loads = [
-        pltpu.make_async_copy(teacher_hbm, teacher, load_sem.at[0]),
-        pltpu.make_async_copy(student_hbm, student, load_sem.at[1]),
+        pltpu.make_async_copy(source, queries.at[at], load_sem)
+        for at, source in enumerate((teacher_hbm, student_hbm))
     ]
     for load in loads:
         load.start()
@@ -93,8 +93,8 @@
         for step in range(heads):
             greet(worker_of(lax.rem(head + heads - 1 - step, heads)))
 
-    for load in loads:
-        load.wait()
+    pltpu.make_async_copy(queries, queries, load_sem).wait()
+    teacher, student = queries.at[0], queries.at[1]
     lane = lax.broadcasted_iota(jnp.int32, (rows, LANES), 1)
     lower = lane < HEAD_DIM
     none = jnp.zeros((), jnp.bfloat16)
@@ -111,7 +111,7 @@
 
     def query_copy(to_head, slot):
         return remote(
-            outbox.at[to_head], inbox.at[slot], send_sem, recv_sem.at[lax.div(slot, 2)],
+            outbox.at[to_head], inbox.at[slot], send_sem, recv_sem.at[lax.div(slot, n // 2)],
             worker_of(to_head),
         )
 
@@ -136,9 +136,10 @@
         return remote(whole, whole, sem, sem, me)
 
     others = [lax.rem(head + way * step + heads, heads) for step in (3, 1, 2)]
+    slots = [place_in(worker_of(to_head)) for to_head in others]
     pl.semaphore_wait(barrier, jnp.where(is_worker, n - 1, heads))
-    for to_head in others:
-        query_copy(to_head, place_in(worker_of(to_head))).start()
+    for to_head, slot in zip(others, slots, strict=True):
+        query_copy(to_head, slot).start()
 
     @pl.when(jnp.logical_not(is_worker))
     def send_near():
@@ -178,8 +179,8 @@
         own_stats[turn, pl.ds(len(lines), 8 - len(lines)), :] = jnp.zeros(
             (8 - len(lines), rows), jnp.float32
         )
-    for to_head in others:
-        stat_copy(to_head, place_in(worker_of(to_head))).start()
+    for to_head, slot in zip(others, slots, strict=True):
+        stat_copy(to_head, slot).start()
     table_load.wait()
 
     @pl.when(jnp.logical_not(is_worker))
@@ -255,21 +256,11 @@
             turned[slot] = block.T[HEAD_DIM:]
             return carry
 
-        def take_chip(shift, carry):
-            if isinstance(shift, int) and shift == 0:
-                all_of(inbox, 1, 1, recv_sem.at[0]).wait_recv()
-            else:
-                all_of(inbox, 2 * shift, 2, recv_sem.at[shift]).wait_recv()
-            for inner in range(2):
-                keep_block(2 * shift + inner, None)
-            return carry
-
-        take_chip(0, None)
-        if chips > 16:
-            lax.fori_loop(1, chips, take_chip, None)
-        else:
-            for shift in range(1, chips):
-                take_chip(shift, None)
+        half = n // 2
+        all_of(inbox, 1, half - 1, recv_sem.at[0]).wait_recv()
+        repeat(half, keep_block)
+        all_of(inbox, half, half, recv_sem.at[1]).wait_recv()
+        repeat(half, lambda step, carry: keep_block(half + step, carry))
 
         def measure_edge(edge, carry):
             t_exp, s_exp, lines = measured(*tile(left[edge_col[edge]], inbox[edge_row[edge]]))
@@ -481,7 +472,6 @@
 def per_device(n, teacher_q, student_q, owner_table):
     rows, width = teacher_q.shape
     heads = width // HEAD_DIM
-    chips = n // 2
     owned = n // heads
     most = 2 * (n * owned - n)
     keep = most * 2 * rows * rows * 4 <= KEEP_BYTES
@@ -496,8 +486,7 @@
         in_specs=[hbm, hbm, hbm],
         out_specs=(vmem, vmem),
         scratch_shapes=[
-            pltpu.VMEM((rows, width), jnp.bfloat16),
-            pltpu.VMEM((rows, width), jnp.bfloat16),
+            pltpu.VMEM((2, rows, width), jnp.bfloat16),
             pltpu.VMEM((heads, rows, LANES), jnp.bfloat16),
             pltpu.VMEM((heads, HEAD_DIM, rows), jnp.bfloat16),
             pltpu.VMEM((heads, 2, rows, rows), jnp.float32),
@@ -524,10 +513,10 @@
             pltpu.VMEM((n, HEAD_DIM, rows), jnp.bfloat16),
             pltpu.VMEM((heads, HEAD_DIM, rows), jnp.bfloat16),
             pltpu.VMEM((heads, HEAD_DIM, rows), jnp.float32),
+            pltpu.SemaphoreType.DMA,
+            pltpu.SemaphoreType.DMA,
+            pltpu.SemaphoreType.DMA,
             pltpu.SemaphoreType.DMA((2,)),
-            pltpu.SemaphoreType.DMA,
-            pltpu.SemaphoreType.DMA,
-            pltpu.SemaphoreType.DMA((chips,)),
             pltpu.SemaphoreType.DMA,
             pltpu.SemaphoreType.DMA,
             pltpu.SemaphoreType.DMA,

time: 12.7 us -> 12.7 us (level)
  no operation moved by 1% of the time
where the time goes in v8:
time: 12.7 us; the launch traced here: 12.5 us
  Pallas kernels  11.9 us (94%)
  between operations  0.64 us (5%)
    pallas_call x1, Pallas kernels, per_device(): pl.pallas_call(functools.partial(kernel, n, most, keep), out_shape=(pltpu...  11.2 us
    pallas_call x1, Pallas kernels, per_device(): pl.pallas_call(unpack, out_shape=(jax.ShapeDtypeStruct((rows, width), jnp...  0.7 us

profile of v8, /device:TPU:0, one launch (start us, length us, event | category | flops | bytes accessed | tf_op | source)
XLA Modules:
  0.0 12.5 jit_solution(13886151272181404550)
XLA Ops:
  0.6 11.2 %distill.1 = (bf16[4,64,128]{2,1,0:T(8,128)(2,1)S(1)}, f32[4,128]{1,0:T(4,128)S(1)}) custom-call(bf16[128,256]{1,0:T(8,128)(2,1)} %teacher_hbm.1, bf16[128,256]{1,0:T(8,128)(2,1)} %student_hbm.1, s32[8,8]{1,0:T(8,128)} %table_hbm.1), custom_call_target="tpu_custom_call" | custom-call | tf_op jit(solution)/shard_map/distill/pallas_call | solution.py:480
  11.8 0.7 %unpack.1 = (bf16[128,256]{1,0:T(8,128)(2,1)}, f32[1,4]{1,0:T(1,128)}) custom-call(bf16[4,64,128]{2,1,0:T(8,128)(2,1)S(1)} %get-tuple-element.6.in_grad, f32[4,128]{1,0:T(4,128)S(1)} %get-tuple-element.7.in_div), custom_call_target="tpu_custom_call" | custom-call | tf_op jit(solution)/shard_map/unpack/pallas_call | solution.py:532

commit v9 on v7

--- a/solution.py
+++ b/solution.py
@@ -135,15 +135,6 @@
         whole = ref.at[pl.ds(first, count)]
         return remote(whole, whole, sem, sem, me)
 
-    others = [lax.rem(head + way * step + heads, heads) for step in (3, 1, 2)]
-    pl.semaphore_wait(barrier, jnp.where(is_worker, n - 1, heads))
-    for to_head in others:
-        query_copy(to_head, place_in(worker_of(to_head))).start()
-
-    @pl.when(jnp.logical_not(is_worker))
-    def send_near():
-        query_copy(head, place_in(worker_of(head))).start()
-
     def masked(block):
         return jnp.where(lower, block, none), jnp.where(lower, none, block)
 
@@ -178,8 +169,18 @@
         own_stats[turn, pl.ds(len(lines), 8 - len(lines)), :] = jnp.zeros(
             (8 - len(lines), rows), jnp.float32
         )
-    for to_head in others:
-        stat_copy(to_head, place_in(worker_of(to_head))).start()
+    others = [lax.rem(head + way * step + heads, heads) for step in (3, 1, 2)]
+    slots = [place_in(worker_of(to_head)) for to_head in others]
+    pl.semaphore_wait(barrier, jnp.where(is_worker, n - 1, heads))
+    for to_head, slot in zip(others, slots, strict=True):
+        query_copy(to_head, slot).start()
+
+    @pl.when(jnp.logical_not(is_worker))
+    def send_near():
+        query_copy(head, place_in(worker_of(head))).start()
+
+    for to_head, slot in zip(others, slots, strict=True):
+        stat_copy(to_head, slot).start()
     table_load.wait()
 
     @pl.when(jnp.logical_not(is_worker))
@@ -398,7 +399,7 @@
             high, low = edge_row[2 * pair], edge_col[2 * pair]
             gap = gap_of(2 * pair, low, high)
             back = gap_of(2 * pair + 1, high, low)
-            symmetric = (gap + back.T).astype(jnp.bfloat16)
+            symmetric = gap.astype(jnp.bfloat16) + back.astype(jnp.bfloat16).T
             shares[2 * pair] = jnp.dot(turned[low], symmetric, preferred_element_type=jnp.float32)
             shares[2 * pair + 1] = lax.dot_general(
                 turned[high], symmetric, (((1,), (1,)), ((), ())),

time: 12.7 us -> 12.7 us (level)
  no operation moved by 1% of the time
where the time goes in v9:
time: 12.7 us; the launch traced here: 12.5 us
  Pallas kernels  11.9 us (94%)
  between operations  0.64 us (5%)
    pallas_call x1, Pallas kernels, per_device(): pl.pallas_call(functools.partial(kernel, n, most, keep), out_shape=(pltpu...  11.2 us
    pallas_call x1, Pallas kernels, per_device(): pl.pallas_call(unpack, out_shape=(jax.ShapeDtypeStruct((rows, width), jnp...  0.7 us

profile of v9, /device:TPU:0, one launch (start us, length us, event | category | flops | bytes accessed | tf_op | source)
XLA Modules:
  0.0 12.5 jit_solution(10104925972573361526)
XLA Ops:
  0.6 11.2 %distill.1 = (bf16[4,64,128]{2,1,0:T(8,128)(2,1)S(1)}, f32[4,128]{1,0:T(4,128)S(1)}) custom-call(bf16[128,256]{1,0:T(8,128)(2,1)} %teacher_hbm.1, bf16[128,256]{1,0:T(8,128)(2,1)} %student_hbm.1, s32[8,8]{1,0:T(8,128)} %table_hbm.1), custom_call_target="tpu_custom_call" | custom-call | tf_op jit(solution)/shard_map/distill/pallas_call | solution.py:491
  11.8 0.7 %unpack.1 = (bf16[128,256]{1,0:T(8,128)(2,1)}, f32[1,4]{1,0:T(1,128)}) custom-call(bf16[4,64,128]{2,1,0:T(8,128)(2,1)S(1)} %get-tuple-element.6.in_grad, f32[4,128]{1,0:T(4,128)S(1)} %get-tuple-element.7.in_div), custom_call_target="tpu_custom_call" | custom-call | tf_op jit(solution)/shard_map/unpack/pallas_call | solution.py:544

commit v10 on v7

--- a/solution.py
+++ b/solution.py
@@ -136,9 +136,10 @@
         return remote(whole, whole, sem, sem, me)
 
     others = [lax.rem(head + way * step + heads, heads) for step in (3, 1, 2)]
+    slots = [place_in(worker_of(to_head)) for to_head in others]
     pl.semaphore_wait(barrier, jnp.where(is_worker, n - 1, heads))
-    for to_head in others:
-        query_copy(to_head, place_in(worker_of(to_head))).start()
+    for to_head, slot in zip(others, slots, strict=True):
+        query_copy(to_head, slot).start()
 
     @pl.when(jnp.logical_not(is_worker))
     def send_near():
@@ -178,8 +179,8 @@
         own_stats[turn, pl.ds(len(lines), 8 - len(lines)), :] = jnp.zeros(
             (8 - len(lines), rows), jnp.float32
         )
-    for to_head in others:
-        stat_copy(to_head, place_in(worker_of(to_head))).start()
+    for to_head, slot in zip(others, slots, strict=True):
+        stat_copy(to_head, slot).start()
     table_load.wait()
 
     @pl.when(jnp.logical_not(is_worker))

time: 12.7 us -> 12.7 us (level)
  no operation moved by 1% of the time
where the time goes in v10:
time: 12.7 us; the launch traced here: 12.5 us
  Pallas kernels  11.9 us (94%)
  between operations  0.64 us (5%)
    pallas_call x1, Pallas kernels, per_device(): pl.pallas_call(functools.partial(kernel, n, most, keep), out_shape=(pltpu...  11.2 us
    pallas_call x1, Pallas kernels, per_device(): pl.pallas_call(unpack, out_shape=(jax.ShapeDtypeStruct((rows, width), jnp...  0.7 us

profile of v10, /device:TPU:0, one launch (start us, length us, event | category | flops | bytes accessed | tf_op | source)
XLA Modules:
  0.0 12.5 jit_solution(6254028641023970056)
XLA Ops:
  0.6 11.2 %distill.1 = (bf16[4,64,128]{2,1,0:T(8,128)(2,1)S(1)}, f32[4,128]{1,0:T(4,128)S(1)}) custom-call(bf16[128,256]{1,0:T(8,128)(2,1)} %teacher_hbm.1, bf16[128,256]{1,0:T(8,128)(2,1)} %student_hbm.1, s32[8,8]{1,0:T(8,128)} %table_hbm.1), custom_call_target="tpu_custom_call" | custom-call | tf_op jit(solution)/shard_map/distill/pallas_call | solution.py:491
  11.8 0.7 %unpack.1 = (bf16[128,256]{1,0:T(8,128)(2,1)}, f32[1,4]{1,0:T(1,128)}) custom-call(bf16[4,64,128]{2,1,0:T(8,128)(2,1)S(1)} %get-tuple-element.6.in_grad, f32[4,128]{1,0:T(4,128)S(1)} %get-tuple-element.7.in_div), custom_call_target="tpu_custom_call" | custom-call | tf_op jit(solution)/shard_map/unpack/pallas_call | solution.py:544
